TPU v7x, 32 devices: a whole 2x2x4 slice. The times are simulated.
32 devices in a mesh: gx: 4 (over y, core), gy: 8 (over z, x).
Axes of the slice: x: 2, y: 2, z: 4, core: 2. Of those that a mesh axis runs over, the one named last changes fastest.
Arguments:
- motion_cotangent: float32 [3, 64, 128, 512], P(None, 'gx', 'gy'), may hold values from -8 to 8
- scaled_warmth: float32 [64, 128, 512], P('gx', 'gy'), may hold values from 0 to 1
- yielding_flags: int32 [64, 128, 512], P('gx', 'gy'), may hold values 0 or 1
- printed_flags: int32 [64, 128, 512], P('gx', 'gy'), may hold values 0 or 1
- material_label: int32 [64, 128, 512], P('gx', 'gy'), may hold values from 0 to 3
- phase_rigidity: float32 [4], replicated, may hold values from 0.5 to 4
- phase_dilatation: float32 [4], replicated, may hold values from 0.5 to 2
- phase_diffusivity: float32 [4], replicated, may hold values from 0.2 to 1
Outputs:
- adjoint_displacement: float32 [3, 64, 128, 512], P(None, 'gx', 'gy')
- thermal_adjoint: float32 [64, 128, 512], P('gx', 'gy')
All inputs are finite; a program needn't handle non-finite values. No bound on the sum of `yielding_flags` or of `printed_flags` on one device may be relied on, other than what follows from the above.
Results may differ from a plain program's by a relative error of at most 0.0001.
Values sent between devices are 32-bit elements; how exact they have to be, the bound alone decides.
No kernel may reach another device: no remote copies, remote signals or barrier semaphores. Data moves between devices by JAX's collectives and lax.ppermute only.
A program may use at most 64 MiB of HBM per device.

v0:
```python
import jax
import jax.numpy as jnp
from jax import lax
from jax.sharding import PartitionSpec as P

ITERS = 2


def with_halo(array, sides, width):
    for axis, dim in sides:
        count, length = (lax.axis_size(axis), array.shape[dim])
        up = [(i, (i + 1) % count) for i in range(count - 1)]
        down = [(j, i) for i, j in up]
        last = lax.slice_in_dim(array, length - width, length, axis=dim)
        leading = lax.slice_in_dim(array, 0, width, axis=dim)
        before = lax.ppermute(last, axis, up)
        after = lax.ppermute(leading, axis, down)
        array = jnp.concatenate([before, array, after], axis=dim)
    return array


def pad_depth(field):
    widths = [(0, 0)] * (field.ndim - 1) + [(1, 1)]
    return jnp.pad(field, widths)


def neighbours(padded):
    return [
        padded[..., 2:, 1:-1, 1:-1],
        padded[..., :-2, 1:-1, 1:-1],
        padded[..., 1:-1, 2:, 1:-1],
        padded[..., 1:-1, :-2, 1:-1],
        padded[..., 1:-1, 1:-1, 2:],
        padded[..., 1:-1, 1:-1, :-2],
    ]


def indexed_values(table, material_label):
    result = jnp.zeros(material_label.shape, jnp.float32)
    for index in range(table.shape[0]):
        result = result + jnp.where(material_label == index, table[index], 0.0)
    return result


def two_products(residual, applied):
    return lax.psum((jnp.sum(residual * residual), jnp.sum(residual * applied)), ("gx", "gy"))


def per_device(
    motion_cotangent,
    scaled_warmth,
    yielding_flags,
    printed_flags,
    material_label,
    phase_rigidity,
    phase_dilatation,
    phase_diffusivity,
):
    hooke_tensor = (
        indexed_values(phase_rigidity, material_label)
        * (1.0 - 0.7 * yielding_flags.astype(jnp.float32))
        * (0.05 + 0.95 * printed_flags.astype(jnp.float32))
    )
    conductance = indexed_values(phase_diffusivity, material_label)
    thermal_scaling = (
        indexed_values(phase_dilatation, material_label) * (0.5 + scaled_warmth) * hooke_tensor
    )
    stacked = jnp.stack([hooke_tensor, conductance])
    coef_pad = pad_depth(with_halo(stacked, (("gx", 1), ("gy", 2)), 1))
    weights = [0.5 * (hooke_tensor + other) for other in neighbours(coef_pad[0])]
    cond_near = neighbours(coef_pad[1])
    diagonal = 0.5 + sum(weights)

    def operate(field):
        padded = pad_depth(with_halo(field, (("gx", 1), ("gy", 2)), 1))
        total = diagonal * field
        for weight, other in zip(weights, neighbours(padded)):
            total = total - weight * other
        return total

    solution = jnp.zeros_like(motion_cotangent)
    residual = motion_cotangent
    applied = operate(residual)
    norm_now, product = two_products(residual, applied)
    step_size = norm_now / product
    direction = residual
    along = applied
    for iteration in range(ITERS):
        solution = solution + step_size * direction
        residual = residual - step_size * along
        if iteration + 1 < ITERS:
            applied = operate(residual)
            norm_next, product = two_products(residual, applied)
            ratio = norm_next / norm_now
            step_size = norm_next / (product - ratio * norm_next / step_size)
            direction = residual + ratio * direction
            along = applied + ratio * along
            norm_now = norm_next
    padded = pad_depth(with_halo(solution, (("gx", 1), ("gy", 2)), 1))
    flux_balance = padded[0, 2:, 1:-1, 1:-1] - padded[0, :-2, 1:-1, 1:-1]
    flux_balance = flux_balance + (padded[1, 1:-1, 2:, 1:-1] - padded[1, 1:-1, :-2, 1:-1])
    flux_balance = flux_balance + (padded[2, 1:-1, 1:-1, 2:] - padded[2, 1:-1, 1:-1, :-2])
    energy_input = -0.5 * thermal_scaling * flux_balance
    source_pad = pad_depth(with_halo(energy_input, (("gx", 0), ("gy", 1)), 1))
    change = jnp.zeros_like(energy_input)
    for other_c, other_s in zip(cond_near, neighbours(source_pad)):
        change = change + 0.5 * (conductance + other_c) * (other_s - energy_input)
    thermal = energy_input + 0.15 * change
    return (solution, thermal)


def solution(mesh):
    in_specs = (
        P(None, "gx", "gy", None),
        P("gx", "gy", None),
        P("gx", "gy", None),
        P("gx", "gy", None),
        P("gx", "gy", None),
        P(),
        P(),
        P(),
    )
    out_specs = (P(None, "gx", "gy", None), P("gx", "gy", None))
    return jax.shard_map(
        per_device, mesh=mesh, in_specs=in_specs, out_specs=out_specs, check_vma=False
    )
```

profile of v0, /device:TPU:9, one launch (start us, length us, event | category | flops | bytes accessed | tf_op | source)
XLA Modules:
  0.0 214.7 jit_solution(2701740574955945685)
XLA Ops:
  3.6 4.1 %fusion.69 = (f32[1,16,16,512]{3,1,2,0:T(8,128)S(1)}, pred[16,16,512]{2,0,1:T(8,128)(4,1)S(1)}, pred[16,16,512]{2,0,1:T(8,128)(4,1)S(1)}, pred[16,16,512]{2,0,1:T(8,128)(4,1)S(1)}, pred[16,16,512]{2,0,1:T(8,128)(4,1)S(1)}) fusion(f32[]{:T(128)} %bitcast.8, f32[]{:T(128)} %bitcast.7, f32[]{:T(128)} %bitcast.6, f32[]{:T(128)} %bitcast.5, s32[16,16,512]{2,1,0:T(8,128)} %param.12), kind=kLoop, calls=%fused_computation.163 | loop fusion | flops 1441792 | bytes 1572880 | tf_op jit(solution)/shard_map/stack | solution.py:68
  7.7 3.4 %fusion.65 = f32[16,16,512]{2,0,1:T(8,128)S(1)} fusion(s32[16,16,512]{2,1,0:T(8,128)S(1)} %copy-done.20, s32[16,16,512]{2,1,0:T(8,128)S(1)} %copy-done.21, pred[16,16,512]{2,0,1:T(8,128)(4,1)S(1)} %get-tuple-element.25, pred[16,16,512]{2,0,1:T(8,128)(4,1)S(1)} %get-tuple-element.24, pred[16,16,512]{2,0,1:T(8,128)(4,1)S(1)} %get-tuple-element.23, ...), kind=kLoop, calls=%fused_computation.152 | loop fusion | flops 1966080 | bytes 2097168 | tf_op jit(solution)/shard_map/mul | solution.py:60
  11.3 3.7 %collective-permute-start = (f32[2,1,16,512]{3,1,2,0:T(1,128)S(1)}, f32[2,1,16,512]{3,1,2,0:T(1,128)S(1)}, u32[]{:S(2)}, u32[]{:S(2)}) collective-permute-start(f32[2,1,16,512]{3,1,2,0:T(1,128)S(1)} %get-tuple-element.42), channel_id=1, source_target_pairs={{0,8},{8,16},{16,24},{1,9},{9,17},{17,25},{2,10},{10,18},{18,26},{... | collective-permute-start | bytes 196616 | tf_op jit(solution)/shard_map/ppermute | solution.py:16
  18.9 3.6 %collective-permute-start.5 = (f32[3,1,16,512]{3,2,1,0:T(8,128)S(1)}, f32[3,1,16,512]{3,2,1,0:T(8,128)S(1)}, u32[]{:S(2)}, u32[]{:S(2)}) collective-permute-start(f32[3,1,16,512]{3,2,1,0:T(8,128)S(1)} %get-tuple-element.38), channel_id=1, source_target_pairs={{0,8},{8,16},{16,24},{1,9},{9,17},{17,25},{2,10},{10,18},{18,26},{... | collective-permute-start | bytes 294920 | tf_op jit(solution)/shard_map/ppermute | solution.py:16
  24.6 3.1 %collective-permute-start.2 = (f32[2,18,1,512]{3,1,2,0:T(8,128)S(1)}, f32[2,18,1,512]{3,1,2,0:T(8,128)S(1)}, u32[]{:S(2)}, u32[]{:S(2)}) collective-permute-start(f32[2,18,1,512]{3,1,2,0:T(8,128)S(1)} %get-tuple-element.40), channel_id=1, source_target_pairs={{0,1},{1,2},{2,3},{3,4},{4,5},{5,6},{6,7},{8,9},{9,10},{10,11},{11... | collective-permute-start | bytes 221192 | tf_op jit(solution)/shard_map/ppermute | solution.py:16
  27.7 3.1 %collective-permute-start.3 = (f32[2,18,1,512]{3,1,2,0:T(8,128)S(1)}, f32[2,18,1,512]{3,1,2,0:T(8,128)S(1)}, u32[]{:S(2)}, u32[]{:S(2)}) collective-permute-start(f32[2,18,1,512]{3,1,2,0:T(8,128)S(1)} %get-tuple-element.41), channel_id=1, source_target_pairs={{1,0},{2,1},{3,2},{4,3},{5,4},{6,5},{7,6},{9,8},{10,9},{11,10},{12... | collective-permute-start | bytes 221192 | tf_op jit(solution)/shard_map/ppermute | solution.py:17
  31.1 2.1 collective-permute-start.6
  33.2 3.2 %collective-permute-start.7 = (f32[3,18,1,512]{3,1,2,0:T(8,128)S(1)}, f32[3,18,1,512]{3,1,2,0:T(8,128)S(1)}, u32[]{:S(2)}, u32[]{:S(2)}) collective-permute-start(f32[3,18,1,512]{3,1,2,0:T(8,128)S(1)} %get-tuple-element.32), channel_id=1, source_target_pairs={{0,1},{1,2},{2,3},{3,4},{4,5},{5,6},{6,7},{8,9},{9,10},{10,11},{11... | collective-permute-start | bytes 331784 | tf_op jit(solution)/shard_map/ppermute | solution.py:16
  39.5 2.2 %collective-permute-done.7 = f32[3,18,1,512]{3,1,2,0:T(8,128)S(1)} collective-permute-done((f32[3,18,1,512]{3,1,2,0:T(8,128)S(1)}, f32[3,18,1,512]{3,1,2,0:T(8,128)S(1)}, u32[]{:S(2)}, u32[]{:S(2)}) %collective-permute-start.7) | collective-permute-done | bytes 110624 | tf_op jit(solution)/shard_map/ppermute | solution.py:16
  41.8 3.2 %select_maximum_fusion.8 = f32[3,18,18,514]{3,1,2,0:T(8,128)S(1)} fusion(f32[3,18,1,512]{3,1,2,0:T(8,128)S(1)} %collective-permute-done.6, f32[3,18,1,512]{3,1,2,0:T(8,128)S(1)} %collective-permute-done.7, f32[3,1,16,512]{3,1,2,0:T(1,128)S(1)} %copy.37, f32[3,16,16,512]{3,1,2,0:T(8,128)S(1)} %copy.43, f32[3,1,16,512]{3,1,2,0:T(1,128)S(1)} %copy.38), kind=kLoop, calls=%fused_computation.10 | loop fusion | flops 5995296 | bytes 3989088 | tf_op jit(solution)/shard_map/concatenate | solution.py:18
  45.1 5.5 %multiply_reduce_fusion.1 = (f32[]{:T(128)}, f32[3,16,16,512]{3,1,2,0:T(8,128)}) fusion(f32[3,16,16,512]{3,2,1,0:T(8,128)S(1)} %copy-done, f32[3,18,18,514]{3,1,2,0:T(8,128)S(1)} %select_maximum_fusion.8, f32[16,16,512]{2,0,1:T(8,128)S(1)} %get-tuple-element.20, f32[16,16,512]{2,0,1:T(8,128)S(1)} %get-tuple-element.19, f32[3,1,16,512]{3,1,2,0:T(1,128)S(1)} %copy.37, ...), kind=kLoop, calls=%fused_computation.70 | loop fusion | flops 9043967 | bytes 11952132 | tf_op jit(solution)/shard_map/reduce_sum | solution.py:46
  50.6 39.0 %all-reduce.6 = (f32[]{:T(128)}, f32[]{:T(128)}) all-reduce(f32[]{:T(128)} %multiply_reduce_fusion.2, f32[]{:T(128)} %get-tuple-element.12), channel_id=1, replica_groups=mesh['gx'=4,'gy'=8] {'gx','gy'}, use_global_device_ids=true, to_apply=%region_1.2 | all-reduce | flops 2 | bytes 16 | tf_op jit(solution)/shard_map/psum | solution.py:46
  90.9 2.9 %multiply_reduce_fusion = (f32[]{:T(128)}, f32[3,16,16,512]{3,1,2,0:T(8,128)S(1)}) fusion(f32[3,16,16,512]{3,1,2,0:T(8,128)} %get-tuple-element.13, f32[]{:T(128)S(6)} %div.12, f32[3,16,16,512]{3,2,1,0:T(8,128)S(1)} %copy-done), kind=kLoop, calls=%fused_computation.68 | loop fusion | flops 1572863 | bytes 4718600 | tf_op jit(solution)/shard_map/reduce_sum | solution.py:46
  94.0 3.1 %collective-permute-start.8 = (f32[3,1,16,512]{3,2,1,0:T(8,128)S(1)}, f32[3,1,16,512]{3,2,1,0:T(8,128)S(1)}, u32[]{:S(2)}, u32[]{:S(2)}) collective-permute-start(f32[3,1,16,512]{3,2,1,0:T(8,128)S(1)} %copy.46), channel_id=1, source_target_pairs={{8,0},{16,8},{24,16},{9,1},{17,9},{25,17},{10,2},{18,10},{26,18},{... | collective-permute-start | bytes 294920 | tf_op jit(solution)/shard_map/ppermute | solution.py:17
  97.2 4.2 %collective-permute-start.9 = (f32[3,1,16,512]{3,2,1,0:T(8,128)S(1)}, f32[3,1,16,512]{3,2,1,0:T(8,128)S(1)}, u32[]{:S(2)}, u32[]{:S(2)}) collective-permute-start(f32[3,1,16,512]{3,2,1,0:T(8,128)S(1)} %copy.48), channel_id=1, source_target_pairs={{0,8},{8,16},{16,24},{1,9},{9,17},{17,25},{2,10},{10,18},{18,26},{... | collective-permute-start | bytes 294920 | tf_op jit(solution)/shard_map/ppermute | solution.py:16
  103.0 3.0 %collective-permute-start.10 = (f32[3,18,1,512]{3,1,2,0:T(8,128)S(1)}, f32[3,18,1,512]{3,1,2,0:T(8,128)S(1)}, u32[]{:S(2)}, u32[]{:S(2)}) collective-permute-start(f32[3,18,1,512]{3,1,2,0:T(8,128)S(1)} %get-tuple-element.31), channel_id=1, source_target_pairs={{1,0},{2,1},{3,2},{4,3},{5,4},{6,5},{7,6},{9,8},{10,9},{11,10},{12... | collective-permute-start | bytes 331784 | tf_op jit(solution)/shard_map/ppermute | solution.py:17
  106.1 2.6 %collective-permute-start.11 = (f32[3,18,1,512]{3,1,2,0:T(8,128)S(1)}, f32[3,18,1,512]{3,1,2,0:T(8,128)S(1)}, u32[]{:S(2)}, u32[]{:S(2)}) collective-permute-start(f32[3,18,1,512]{3,1,2,0:T(8,128)S(1)} %get-tuple-element.30), channel_id=1, source_target_pairs={{0,1},{1,2},{2,3},{3,4},{4,5},{5,6},{6,7},{8,9},{9,10},{10,11},{11... | collective-permute-start | bytes 331784 | tf_op jit(solution)/shard_map/ppermute | solution.py:16
  108.9 5.1 %collective-permute-done.11 = f32[3,18,1,512]{3,1,2,0:T(8,128)S(1)} collective-permute-done((f32[3,18,1,512]{3,1,2,0:T(8,128)S(1)}, f32[3,18,1,512]{3,1,2,0:T(8,128)S(1)}, u32[]{:S(2)}, u32[]{:S(2)}) %collective-permute-start.11) | collective-permute-done | bytes 110624 | tf_op jit(solution)/shard_map/ppermute | solution.py:16
  114.0 3.2 %select_maximum_fusion.4 = f32[3,18,18,514]{3,1,2,0:T(8,128)S(1)} fusion(f32[3,18,1,512]{3,1,2,0:T(8,128)S(1)} %collective-permute-done.10, f32[3,18,1,512]{3,1,2,0:T(8,128)S(1)} %collective-permute-done.11, f32[3,1,16,512]{3,1,2,0:T(1,128)S(1)} %copy.47, f32[3,16,16,512]{3,1,2,0:T(8,128)S(1)} %get-tuple-element.11, f32[3,1,16,512]{3,1,2,0:T(1,128)S(1)} %copy.49), kind=kLoop, calls=%fused_computation.6 | loop fusion | flops 5995296 | bytes 3989088 | tf_op jit(solution)/shard_map/concatenate | solution.py:18
  117.3 3.3 %fusion.4 = f32[]{:T(128)} fusion(f32[3,16,16,512]{3,1,2,0:T(8,128)S(1)} %get-tuple-element.11, f32[3,18,18,514]{3,1,2,0:T(8,128)S(1)} %select_maximum_fusion.4, f32[3,18,1,512]{3,1,2,0:T(8,128)S(1)} %collective-permute-done.11, f32[3,1,16,512]{3,1,2,0:T(1,128)S(1)} %copy.47, f32[3,1,16,512]{3,1,2,0:T(1,128)S(1)} %copy.49, ...), kind=kLoop, calls=%fused_computation.28 | loop fusion | flops 9043967 | bytes 8806404 | tf_op jit(solution)/shard_map/reduce_sum | solution.py:46
  120.6 38.9 %all-reduce.5 = (f32[]{:T(128)}, f32[]{:T(128)}) all-reduce(f32[]{:T(128)} %get-tuple-element.10, f32[]{:T(128)} %fusion.4), channel_id=1, replica_groups=mesh['gx'=4,'gy'=8] {'gx','gy'}, use_global_device_ids=true, to_apply=%region_5.6 | all-reduce | flops 2 | bytes 16 | tf_op jit(solution)/shard_map/psum | solution.py:46
  165.4 3.2 %collective-permute-start.12 = (f32[3,1,16,512]{3,2,1,0:T(8,128)S(1)}, f32[3,1,16,512]{3,2,1,0:T(8,128)S(1)}, u32[]{:S(2)}, u32[]{:S(2)}) collective-permute-start(f32[3,1,16,512]{3,2,1,0:T(8,128)S(1)} %copy.54), channel_id=1, source_target_pairs={{8,0},{16,8},{24,16},{9,1},{17,9},{25,17},{10,2},{18,10},{26,18},{... | collective-permute-start | bytes 294920 | tf_op jit(solution)/shard_map/ppermute | solution.py:17
  168.7 4.0 %collective-permute-start.13 = (f32[3,1,16,512]{3,2,1,0:T(8,128)S(1)}, f32[3,1,16,512]{3,2,1,0:T(8,128)S(1)}, u32[]{:S(2)}, u32[]{:S(2)}) collective-permute-start(f32[3,1,16,512]{3,2,1,0:T(8,128)S(1)} %copy.56), channel_id=1, source_target_pairs={{0,8},{8,16},{16,24},{1,9},{9,17},{17,25},{2,10},{10,18},{18,26},{... | collective-permute-start | bytes 294920 | tf_op jit(solution)/shard_map/ppermute | solution.py:16
  174.4 4.2 %collective-permute-start.14 = (f32[3,18,1,512]{3,1,2,0:T(8,128)S(1)}, f32[3,18,1,512]{3,1,2,0:T(8,128)S(1)}, u32[]{:S(2)}, u32[]{:S(2)}) collective-permute-start(f32[3,18,1,512]{3,1,2,0:T(8,128)S(1)} %get-tuple-element.29), channel_id=1, source_target_pairs={{1,0},{2,1},{3,2},{4,3},{5,4},{6,5},{7,6},{9,8},{10,9},{11,10},{12... | collective-permute-start | bytes 331784 | tf_op jit(solution)/shard_map/ppermute | solution.py:17
  181.3 4.6 %collective-permute-done.15 = f32[3,18,1,512]{3,1,2,0:T(8,128)S(1)} collective-permute-done((f32[3,18,1,512]{3,1,2,0:T(8,128)S(1)}, f32[3,18,1,512]{3,1,2,0:T(8,128)S(1)}, u32[]{:S(2)}, u32[]{:S(2)}) %collective-permute-start.15) | collective-permute-done | bytes 110624 | tf_op jit(solution)/shard_map/ppermute | solution.py:16
  185.8 3.2 %select_maximum_fusion = f32[3,18,18,514]{3,1,2,0:T(8,128)S(1)} fusion(f32[3,18,1,512]{3,1,2,0:T(8,128)S(1)} %collective-permute-done.14, f32[3,18,1,512]{3,1,2,0:T(8,128)S(1)} %collective-permute-done.15, f32[3,1,16,512]{3,1,2,0:T(1,128)S(1)} %copy.55, f32[3,16,16,512]{3,1,2,0:T(8,128)S(1)} %multiply_add_fusion, f32[3,1,16,512]{3,1,2,0:T(1,128)S(1)} %copy.57), kind=kLoop, calls=%fused_computation.2 | loop fusion | flops 5995296 | bytes 3989088 | tf_op jit(solution)/shard_map/concatenate | solution.py:18
  189.1 3.5 %fusion.50 = f32[16,16,512]{2,0,1:T(8,128)S(1)} fusion(f32[3,18,18,514]{3,1,2,0:T(8,128)S(1)} %select_maximum_fusion, f32[3,18,1,512]{3,1,2,0:T(8,128)S(1)} %collective-permute-done.15, f32[3,1,16,512]{3,1,2,0:T(1,128)S(1)} %copy.55, f32[3,16,16,512]{3,1,2,0:T(8,128)S(1)} %multiply_add_fusion, f32[3,1,16,512]{3,1,2,0:T(1,128)S(1)} %copy.57, ...), kind=kLoop, calls=%fused_computation.121 | loop fusion | flops 3276800 | bytes 5136400 | tf_op jit(solution)/shard_map/mul | solution.py:103
  192.7 1.9 collective-permute-start.16
  194.6 5.3 %collective-permute-start.17 = (f32[1,16,512]{2,0,1:T(1,128)S(1)}, f32[1,16,512]{2,0,1:T(1,128)S(1)}, u32[]{:S(2)}, u32[]{:S(2)}) collective-permute-start(f32[1,16,512]{2,0,1:T(1,128)S(1)} %get-tuple-element.46), channel_id=1, source_target_pairs={{0,8},{8,16},{16,24},{1,9},{9,17},{17,25},{2,10},{10,18},{18,26},{... | collective-permute-start | bytes 98312 | tf_op jit(solution)/shard_map/ppermute | solution.py:16
  202.9 3.6 %collective-permute-start.19 = (f32[18,1,512]{2,0,1:T(8,128)S(1)}, f32[18,1,512]{2,0,1:T(8,128)S(1)}, u32[]{:S(2)}, u32[]{:S(2)}) collective-permute-start(f32[18,1,512]{2,0,1:T(8,128)S(1)} %get-tuple-element.44), channel_id=1, source_target_pairs={{0,1},{1,2},{2,3},{3,4},{4,5},{5,6},{6,7},{8,9},{9,10},{10,11},{11... | collective-permute-start | bytes 110600 | tf_op jit(solution)/shard_map/ppermute | solution.py:16
  206.5 2.1 copy.60
  209.8 3.8 %fusion.28 = f32[16,16,512]{2,0,1:T(8,128)S(1)} fusion(f32[16,16,512]{2,0,1:T(8,128)S(1)} %fusion.50, f32[18,18,514]{2,0,1:T(8,128)S(1)} %select_maximum_fusion.17, f32[18,18,514]{2,0,1:T(8,128)S(1)} %copy-done.3, f32[18,1,512]{2,0,1:T(8,128)S(1)} %collective-permute-done.19, f32[1,16,512]{2,0,1:T(1,128)S(1)} %collective-permute-done.16, ...), kind=kLoop, calls=%fused_computation.83 | loop fusion | flops 6029312 | bytes 5906448 | tf_op jit(solution)/shard_map/add | solution.py:108
  (100 shorter events, 25.3 us)
Async XLA Ops:
  7.7 9.2 %copy-start = (f32[3,16,16,512]{3,2,1,0:T(8,128)S(1)}, f32[3,16,16,512]{3,2,1,0:T(8,128)}, u32[]{:S(2)}) copy-start(f32[3,16,16,512]{3,2,1,0:T(8,128)} %param.8) | copy-start | bytes 4718596
  11.1 27.6 %copy-start.1 = (f32[16,16,512]{2,0,1:T(8,128)}, f32[16,16,512]{2,0,1:T(8,128)S(1)}, u32[]{:S(2)}) copy-start(f32[16,16,512]{2,0,1:T(8,128)S(1)} %fusion.65) | copy-start | bytes 1572868
  11.3 13.3 %collective-permute-start = (f32[2,1,16,512]{3,1,2,0:T(1,128)S(1)}, f32[2,1,16,512]{3,1,2,0:T(1,128)S(1)}, u32[]{:S(2)}, u32[]{:S(2)}) collective-permute-start(f32[2,1,16,512]{3,1,2,0:T(1,128)S(1)} %get-tuple-element.42), channel_id=1, source_target_pairs={{0,8},{8,16},{16,24},{1,9},{9,17},{17,25},{2,10},{10,18},{18,26},{... | collective-permute-start | bytes 196616 | tf_op jit(solution)/shard_map/ppermute | solution.py:16
  15.0 9.6 %collective-permute-start.1 = (f32[2,1,16,512]{3,1,2,0:T(1,128)S(1)}, f32[2,1,16,512]{3,1,2,0:T(1,128)S(1)}, u32[]{:S(2)}, u32[]{:S(2)}) collective-permute-start(f32[2,1,16,512]{3,1,2,0:T(1,128)S(1)} %get-tuple-element.43), channel_id=1, source_target_pairs={{8,0},{16,8},{24,16},{9,1},{17,9},{25,17},{10,2},{18,10},{26,18},{... | collective-permute-start | bytes 196616 | tf_op jit(solution)/shard_map/ppermute | solution.py:17
  17.0 13.8 %collective-permute-start.4 = (f32[3,1,16,512]{3,2,1,0:T(8,128)S(1)}, f32[3,1,16,512]{3,2,1,0:T(8,128)S(1)}, u32[]{:S(2)}, u32[]{:S(2)}) collective-permute-start(f32[3,1,16,512]{3,2,1,0:T(8,128)S(1)} %get-tuple-element.39), channel_id=1, source_target_pairs={{8,0},{16,8},{24,16},{9,1},{17,9},{25,17},{10,2},{18,10},{26,18},{... | collective-permute-start | bytes 294920 | tf_op jit(solution)/shard_map/ppermute | solution.py:17
  18.9 12.0 %collective-permute-start.5 = (f32[3,1,16,512]{3,2,1,0:T(8,128)S(1)}, f32[3,1,16,512]{3,2,1,0:T(8,128)S(1)}, u32[]{:S(2)}, u32[]{:S(2)}) collective-permute-start(f32[3,1,16,512]{3,2,1,0:T(8,128)S(1)} %get-tuple-element.38), channel_id=1, source_target_pairs={{0,8},{8,16},{16,24},{1,9},{9,17},{17,25},{2,10},{10,18},{18,26},{... | collective-permute-start | bytes 294920 | tf_op jit(solution)/shard_map/ppermute | solution.py:16
  24.6 11.8 %collective-permute-start.2 = (f32[2,18,1,512]{3,1,2,0:T(8,128)S(1)}, f32[2,18,1,512]{3,1,2,0:T(8,128)S(1)}, u32[]{:S(2)}, u32[]{:S(2)}) collective-permute-start(f32[2,18,1,512]{3,1,2,0:T(8,128)S(1)} %get-tuple-element.40), channel_id=1, source_target_pairs={{0,1},{1,2},{2,3},{3,4},{4,5},{5,6},{6,7},{8,9},{9,10},{10,11},{11... | collective-permute-start | bytes 221192 | tf_op jit(solution)/shard_map/ppermute | solution.py:16
  27.7 8.7 %collective-permute-start.3 = (f32[2,18,1,512]{3,1,2,0:T(8,128)S(1)}, f32[2,18,1,512]{3,1,2,0:T(8,128)S(1)}, u32[]{:S(2)}, u32[]{:S(2)}) collective-permute-start(f32[2,18,1,512]{3,1,2,0:T(8,128)S(1)} %get-tuple-element.41), channel_id=1, source_target_pairs={{1,0},{2,1},{3,2},{4,3},{5,4},{6,5},{7,6},{9,8},{10,9},{11,10},{12... | collective-permute-start | bytes 221192 | tf_op jit(solution)/shard_map/ppermute | solution.py:17
  31.1 8.5 %collective-permute-start.6 = (f32[3,18,1,512]{3,1,2,0:T(8,128)S(1)}, f32[3,18,1,512]{3,1,2,0:T(8,128)S(1)}, u32[]{:S(2)}, u32[]{:S(2)}) collective-permute-start(f32[3,18,1,512]{3,1,2,0:T(8,128)S(1)} %get-tuple-element.33), channel_id=1, source_target_pairs={{1,0},{2,1},{3,2},{4,3},{5,4},{6,5},{7,6},{9,8},{10,9},{11,10},{12... | collective-permute-start | bytes 331784 | tf_op jit(solution)/shard_map/ppermute | solution.py:17
  33.2 8.6 %collective-permute-start.7 = (f32[3,18,1,512]{3,1,2,0:T(8,128)S(1)}, f32[3,18,1,512]{3,1,2,0:T(8,128)S(1)}, u32[]{:S(2)}, u32[]{:S(2)}) collective-permute-start(f32[3,18,1,512]{3,1,2,0:T(8,128)S(1)} %get-tuple-element.32), channel_id=1, source_target_pairs={{0,1},{1,2},{2,3},{3,4},{4,5},{5,6},{6,7},{8,9},{9,10},{10,11},{11... | collective-permute-start | bytes 331784 | tf_op jit(solution)/shard_map/ppermute | solution.py:16
  94.0 7.6 %collective-permute-start.8 = (f32[3,1,16,512]{3,2,1,0:T(8,128)S(1)}, f32[3,1,16,512]{3,2,1,0:T(8,128)S(1)}, u32[]{:S(2)}, u32[]{:S(2)}) collective-permute-start(f32[3,1,16,512]{3,2,1,0:T(8,128)S(1)} %copy.46), channel_id=1, source_target_pairs={{8,0},{16,8},{24,16},{9,1},{17,9},{25,17},{10,2},{18,10},{26,18},{... | collective-permute-start | bytes 294920 | tf_op jit(solution)/shard_map/ppermute | solution.py:17
  97.2 5.7 %collective-permute-start.9 = (f32[3,1,16,512]{3,2,1,0:T(8,128)S(1)}, f32[3,1,16,512]{3,2,1,0:T(8,128)S(1)}, u32[]{:S(2)}, u32[]{:S(2)}) collective-permute-start(f32[3,1,16,512]{3,2,1,0:T(8,128)S(1)} %copy.48), channel_id=1, source_target_pairs={{0,8},{8,16},{16,24},{1,9},{9,17},{17,25},{2,10},{10,18},{18,26},{... | collective-permute-start | bytes 294920 | tf_op jit(solution)/shard_map/ppermute | solution.py:16
  103.0 5.9 %collective-permute-start.10 = (f32[3,18,1,512]{3,1,2,0:T(8,128)S(1)}, f32[3,18,1,512]{3,1,2,0:T(8,128)S(1)}, u32[]{:S(2)}, u32[]{:S(2)}) collective-permute-start(f32[3,18,1,512]{3,1,2,0:T(8,128)S(1)} %get-tuple-element.31), channel_id=1, source_target_pairs={{1,0},{2,1},{3,2},{4,3},{5,4},{6,5},{7,6},{9,8},{10,9},{11,10},{12... | collective-permute-start | bytes 331784 | tf_op jit(solution)/shard_map/ppermute | solution.py:17
  106.0 11.2 %copy-start.5 = (f32[16,16,512]{2,0,1:T(8,128)S(1)}, f32[16,16,512]{2,0,1:T(8,128)}, u32[]{:S(2)}) copy-start(f32[16,16,512]{2,0,1:T(8,128)} %copy-done.4) | copy-start | bytes 1572868
  106.0 11.2 %copy-start.7 = (f32[16,16,512]{2,0,1:T(8,128)S(1)}, f32[16,16,512]{2,0,1:T(8,128)}, u32[]{:S(2)}) copy-start(f32[16,16,512]{2,0,1:T(8,128)} %copy-done.6) | copy-start | bytes 1572868
  106.0 11.2 %copy-start.9 = (f32[16,16,512]{2,0,1:T(8,128)S(1)}, f32[16,16,512]{2,0,1:T(8,128)}, u32[]{:S(2)}) copy-start(f32[16,16,512]{2,0,1:T(8,128)} %copy-done.8) | copy-start | bytes 1572868
  106.0 11.2 %copy-start.11 = (f32[16,16,512]{2,0,1:T(8,128)S(1)}, f32[16,16,512]{2,0,1:T(8,128)}, u32[]{:S(2)}) copy-start(f32[16,16,512]{2,0,1:T(8,128)} %copy-done.10) | copy-start | bytes 1572868
  106.0 11.2 %copy-start.13 = (f32[16,16,512]{2,0,1:T(8,128)S(1)}, f32[16,16,512]{2,0,1:T(8,128)}, u32[]{:S(2)}) copy-start(f32[16,16,512]{2,0,1:T(8,128)} %copy-done.12) | copy-start | bytes 1572868
  106.0 11.2 %copy-start.15 = (f32[16,16,512]{2,0,1:T(8,128)S(1)}, f32[16,16,512]{2,0,1:T(8,128)}, u32[]{:S(2)}) copy-start(f32[16,16,512]{2,0,1:T(8,128)} %copy-done.14) | copy-start | bytes 1572868
  106.1 11.2 %copy-start.17 = (f32[16,16,512]{2,0,1:T(8,128)S(1)}, f32[16,16,512]{2,0,1:T(8,128)}, u32[]{:S(2)}) copy-start(f32[16,16,512]{2,0,1:T(8,128)} %copy-done.16) | copy-start | bytes 1572868
  106.1 7.9 %collective-permute-start.11 = (f32[3,18,1,512]{3,1,2,0:T(8,128)S(1)}, f32[3,18,1,512]{3,1,2,0:T(8,128)S(1)}, u32[]{:S(2)}, u32[]{:S(2)}) collective-permute-start(f32[3,18,1,512]{3,1,2,0:T(8,128)S(1)} %get-tuple-element.30), channel_id=1, source_target_pairs={{0,1},{1,2},{2,3},{3,4},{4,5},{5,6},{6,7},{8,9},{9,10},{10,11},{11... | collective-permute-start | bytes 331784 | tf_op jit(solution)/shard_map/ppermute | solution.py:16
  165.2 15.4 %copy-start.23 = (f32[4]{0:T(128)S(1)}, f32[4]{0:T(128)}, u32[]{:S(2)}) copy-start(f32[4]{0:T(128)} %param.14) | copy-start | bytes 52
  165.4 7.6 %collective-permute-start.12 = (f32[3,1,16,512]{3,2,1,0:T(8,128)S(1)}, f32[3,1,16,512]{3,2,1,0:T(8,128)S(1)}, u32[]{:S(2)}, u32[]{:S(2)}) collective-permute-start(f32[3,1,16,512]{3,2,1,0:T(8,128)S(1)} %copy.54), channel_id=1, source_target_pairs={{8,0},{16,8},{24,16},{9,1},{17,9},{25,17},{10,2},{18,10},{26,18},{... | collective-permute-start | bytes 294920 | tf_op jit(solution)/shard_map/ppermute | solution.py:17
  168.7 5.6 %collective-permute-start.13 = (f32[3,1,16,512]{3,2,1,0:T(8,128)S(1)}, f32[3,1,16,512]{3,2,1,0:T(8,128)S(1)}, u32[]{:S(2)}, u32[]{:S(2)}) collective-permute-start(f32[3,1,16,512]{3,2,1,0:T(8,128)S(1)} %copy.56), channel_id=1, source_target_pairs={{0,8},{8,16},{16,24},{1,9},{9,17},{17,25},{2,10},{10,18},{18,26},{... | collective-permute-start | bytes 294920 | tf_op jit(solution)/shard_map/ppermute | solution.py:16
  174.4 6.8 %collective-permute-start.14 = (f32[3,18,1,512]{3,1,2,0:T(8,128)S(1)}, f32[3,18,1,512]{3,1,2,0:T(8,128)S(1)}, u32[]{:S(2)}, u32[]{:S(2)}) collective-permute-start(f32[3,18,1,512]{3,1,2,0:T(8,128)S(1)} %get-tuple-element.29), channel_id=1, source_target_pairs={{1,0},{2,1},{3,2},{4,3},{5,4},{6,5},{7,6},{9,8},{10,9},{11,10},{12... | collective-permute-start | bytes 331784 | tf_op jit(solution)/shard_map/ppermute | solution.py:17
  178.7 7.2 %collective-permute-start.15 = (f32[3,18,1,512]{3,1,2,0:T(8,128)S(1)}, f32[3,18,1,512]{3,1,2,0:T(8,128)S(1)}, u32[]{:S(2)}, u32[]{:S(2)}) collective-permute-start(f32[3,18,1,512]{3,1,2,0:T(8,128)S(1)} %get-tuple-element.28), channel_id=1, source_target_pairs={{0,1},{1,2},{2,3},{3,4},{4,5},{5,6},{6,7},{8,9},{9,10},{10,11},{11... | collective-permute-start | bytes 331784 | tf_op jit(solution)/shard_map/ppermute | solution.py:16
  181.3 7.8 %copy-start.19 = (pred[16,16,512]{2,0,1:T(8,128)(4,1)S(1)}, pred[16,16,512]{2,0,1:T(8,128)(4,1)}, u32[]{:S(2)}) copy-start(pred[16,16,512]{2,0,1:T(8,128)(4,1)} %copy-done.18) | copy-start | bytes 393220
  181.3 7.8 %copy-start.22 = (f32[16,16,512]{2,1,0:T(8,128)S(1)}, f32[16,16,512]{2,1,0:T(8,128)}, u32[]{:S(2)}) copy-start(f32[16,16,512]{2,1,0:T(8,128)} %param.9) | copy-start | bytes 1572868
  192.7 7.3 %collective-permute-start.16 = (f32[1,16,512]{2,0,1:T(1,128)S(1)}, f32[1,16,512]{2,0,1:T(1,128)S(1)}, u32[]{:S(2)}, u32[]{:S(2)}) collective-permute-start(f32[1,16,512]{2,0,1:T(1,128)S(1)} %get-tuple-element.47), channel_id=1, source_target_pairs={{8,0},{16,8},{24,16},{9,1},{17,9},{25,17},{10,2},{18,10},{26,18},{... | collective-permute-start | bytes 98312 | tf_op jit(solution)/shard_map/ppermute | solution.py:17
  194.6 6.4 %collective-permute-start.17 = (f32[1,16,512]{2,0,1:T(1,128)S(1)}, f32[1,16,512]{2,0,1:T(1,128)S(1)}, u32[]{:S(2)}, u32[]{:S(2)}) collective-permute-start(f32[1,16,512]{2,0,1:T(1,128)S(1)} %get-tuple-element.46), channel_id=1, source_target_pairs={{0,8},{8,16},{16,24},{1,9},{9,17},{17,25},{2,10},{10,18},{18,26},{... | collective-permute-start | bytes 98312 | tf_op jit(solution)/shard_map/ppermute | solution.py:16
  201.0 7.6 %collective-permute-start.18 = (f32[18,1,512]{2,0,1:T(8,128)S(1)}, f32[18,1,512]{2,0,1:T(8,128)S(1)}, u32[]{:S(2)}, u32[]{:S(2)}) collective-permute-start(f32[18,1,512]{2,0,1:T(8,128)S(1)} %get-tuple-element.45), channel_id=1, source_target_pairs={{1,0},{2,1},{3,2},{4,3},{5,4},{6,5},{7,6},{9,8},{10,9},{11,10},{12... | collective-permute-start | bytes 110600 | tf_op jit(solution)/shard_map/ppermute | solution.py:17
  202.9 5.7 %collective-permute-start.19 = (f32[18,1,512]{2,0,1:T(8,128)S(1)}, f32[18,1,512]{2,0,1:T(8,128)S(1)}, u32[]{:S(2)}, u32[]{:S(2)}) collective-permute-start(f32[18,1,512]{2,0,1:T(8,128)S(1)} %get-tuple-element.44), channel_id=1, source_target_pairs={{0,1},{1,2},{2,3},{3,4},{4,5},{5,6},{6,7},{8,9},{9,10},{10,11},{11... | collective-permute-start | bytes 110600 | tf_op jit(solution)/shard_map/ppermute | solution.py:16
  (12 other events, 65.5 us)
where the time goes:
time: 217 us; the launch traced here: 215 us
  blocking collectives  77.8 us (36%)
  starting transfers between devices  61.7 us (28%)
  other arithmetic  41.2 us (19%)
  waiting for transfers between devices  16.1 us (7%)
  local copies, waits for them, and re-layouts  10.6 us (5%)
  between operations  7.38 us (3%)
    psum x2, blocking collectives, two_products(): lax.psum((jnp.sum(residual * residual), jnp.sum(residual * applied)), ('g...  77.8 us
    ppermute x10, starting transfers between devices, with_halo(): before = lax.ppermute(last, axis, up)  35.3 us
    ppermute x10, starting transfers between devices, with_halo(): after = lax.ppermute(leading, axis, down)  26.4 us
    ppermute x10, waiting for transfers between devices, with_halo(): before = lax.ppermute(last, axis, up)  15.3 us
    concatenate x9, other arithmetic, with_halo(): array = jnp.concatenate([before, array, after], axis=dim)  11.5 us
    reduce_sum x2, other arithmetic, two_products(): jnp.sum(residual * applied)  8.84 us
    unnamed x51, local copies, waits for them, and re-layouts  4.77 us
  transfers between devices with their start and end apart: 20, of which 10 were waited for; matrix products, arithmetic and copies ran while one was open for 4% of the time, Pallas kernels for 0%

commit v1 on v0

v1 whole, which is shorter than its diff:
```python
import jax
import jax.numpy as jnp
from jax import lax
from jax.sharding import PartitionSpec as P

AXES = ("gx", "gy")


def exchange(array, axis, dim):
    count, length = lax.axis_size(axis), array.shape[dim]
    up = [(i, i + 1) for i in range(count - 1)]
    down = [(i + 1, i) for i in range(count - 1)]
    before = lax.ppermute(lax.slice_in_dim(array, length - 1, length, axis=dim), axis, up)
    after = lax.ppermute(lax.slice_in_dim(array, 0, 1, axis=dim), axis, down)
    return before, after


def shifted(array, halo, dim):
    before, after = halo
    length = array.shape[dim]
    inner_up = lax.slice_in_dim(array, 1, length, axis=dim)
    inner_down = lax.slice_in_dim(array, 0, length - 1, axis=dim)
    return (
        jnp.concatenate([inner_up, after], axis=dim),
        jnp.concatenate([before, inner_down], axis=dim),
    )


def depth_halo(array):
    zero = jnp.zeros_like(array[..., :1])
    return zero, zero


def six(array, x_halo, y_halo):
    ndim = array.ndim
    return (
        shifted(array, x_halo, ndim - 3)
        + shifted(array, y_halo, ndim - 2)
        + shifted(array, depth_halo(array), ndim - 1)
    )


def indexed_values(table, label):
    result = jnp.zeros(label.shape, jnp.float32)
    for index in range(table.shape[0]):
        result = result + jnp.where(label == index, table[index], 0.0)
    return result


def cut(halo, where):
    return tuple(part[where] for part in halo)


def per_device(motion, warmth, yielding, printed, label, rigidity, dilatation, diffusivity):
    stiffness = (
        indexed_values(rigidity, label)
        * (1.0 - 0.7 * yielding.astype(jnp.float32))
        * (0.05 + 0.95 * printed.astype(jnp.float32))
    )
    conductance = indexed_values(diffusivity, label)
    scaling = -0.5 * indexed_values(dilatation, label) * (0.5 + warmth) * stiffness
    first = jnp.concatenate([motion, stiffness[None], conductance[None]], axis=0)
    x_first, y_first = exchange(first, "gx", 1), exchange(first, "gy", 2)
    weights = [0.5 * (stiffness + o) for o in six(stiffness, cut(x_first, 3), cut(y_first, 3))]
    diagonal = 0.5 + sum(weights)
    links = [0.5 * (conductance + o) for o in six(conductance, cut(x_first, 4), cut(y_first, 4))]

    def operate(field, x_halo, y_halo):
        total = diagonal * field
        for weight, other in zip(weights, six(field, x_halo, y_halo)):
            total = total - weight * other
        return total

    three = slice(0, 3)
    x_motion, y_motion = cut(x_first, three), cut(y_first, three)
    q = operate(motion, x_motion, y_motion)
    x_q, y_q = exchange(q, "gx", 1), exchange(q, "gy", 2)
    z = operate(q, x_q, y_q)
    dot = lambda a, b: jnp.sum(a * b)
    rr, rq, qq, qz = dot(motion, motion), dot(motion, q), dot(q, q), dot(q, z)
    shift = jnp.where(qq > 0, rq / jnp.where(qq > 0, qq, 1.0), 0.0)
    u = motion - shift * q
    row = jnp.stack([rr, rq, qq, qz, shift, dot(u, u), dot(u, q), dot(u, z)])
    count = lax.axis_size(AXES)
    rows = lax.all_to_all(jnp.broadcast_to(row[None], (count, 8)), AXES, 0, 0)
    rr, rq, qq, qz, shift, uu, uq, uz = [rows[:, i] for i in range(8)]
    total_rr = jnp.sum(rr)
    step = total_rr / jnp.sum(rq)
    gap = step - shift
    next_rr = jnp.sum(uu - 2.0 * gap * uq + gap * gap * qq)
    energy = jnp.sum(
        (uq - shift * uz) - gap * (uz + qq - shift * qz) + gap * gap * qz
    )
    ratio = next_rr / total_rr
    next_step = next_rr / (energy - ratio * next_rr / step)
    c0 = step + next_step * (1.0 + ratio)
    c1 = -next_step * step
    solution = c0 * motion + c1 * q

    def divergence(field, x_halo, y_halo):
        x_up, x_down = shifted(field[0], cut(x_halo, 0), 0)
        y_up, y_down = shifted(field[1], cut(y_halo, 1), 1)
        z_up, z_down = shifted(field[2], depth_halo(field[2]), 2)
        return (x_up - x_down) + (y_up - y_down) + (z_up - z_down)

    sources = jnp.stack(
        [scaling * divergence(motion, x_motion, y_motion), scaling * divergence(q, x_q, y_q)]
    )
    x_s, y_s = exchange(sources, "gx", 1), exchange(sources, "gy", 2)
    mix = lambda pair: c0 * pair[0] + c1 * pair[1]
    source = mix(sources)
    change = jnp.zeros_like(source)
    near = six(source, tuple(map(mix, x_s)), tuple(map(mix, y_s)))
    for link, other in zip(links, near):
        change = change + link * (other - source)
    return solution, source + 0.15 * change


def solution(mesh):
    field = P("gx", "gy", None)
    in_specs = (P(None, "gx", "gy", None), field, field, field, field, P(), P(), P())
    out_specs = (P(None, "gx", "gy", None), field)
    return jax.shard_map(
        per_device, mesh=mesh, in_specs=in_specs, out_specs=out_specs, check_vma=False
    )
```

time: 217 us -> 120 us (0.55)
  blocking collectives: 77.8 us -> 0 us
  starting transfers between devices: 61.7 us -> 39.4 us
  local copies, waits for them, and re-layouts: 10.6 us -> 32.9 us
  other arithmetic: 41.2 us -> 30 us
  waiting for transfers between devices: 16.1 us -> 8.53 us
    psum x2 -> x0, blocking collectives: 77.8 us -> none  [two_products(): lax.psum((jnp.sum(residual * residual), jnp.sum(residual * applied)), ('g...]
    ppermute x20 -> x12, starting transfers between devices: 61.7 us -> 34.8 us  [the longest x6 20 us: exchange(): lax.ppermute(lax.slice_in_dim(array, length - 1, length, axis=dim), axis,...]
    slice x11 -> x30, local copies, waits for them, and re-layouts: 4.04 us -> 24.4 us  [the longest x12 11.5 us: shifted(): inner_up = lax.slice_in_dim(array, 1, length, axis=dim)]
    ppermute x20 -> x12, waiting for transfers between devices: 16.1 us -> 3.55 us  [the longest x6 3.53 us: exchange(): after = lax.ppermute(lax.slice_in_dim(array, 0, 1, axis=dim), axis, down)]
    concatenate x9 -> x1, other arithmetic: 11.5 us -> 0.32 us  [per_device(): jnp.concatenate([motion, stiffness[None], conductance[None]], axis=0)]
    add x2 -> x8, other arithmetic: 4.93 us -> 10.1 us  [the longest x5 3.95 us: per_device(): mix = lambda pair: c0 * pair[0] + c1 * pair[1]]
    all_to_all x0 -> x1, waiting for transfers between devices: none -> 4.98 us  [per_device(): rows = lax.all_to_all(jnp.broadcast_to(row[None], (count, 8)), AXES, 0, 0)]
    unnamed x51 -> x40, local copies, waits for them, and re-layouts: 4.77 us -> 0.08 us
  transfers between devices with their start and end apart: 20 -> 13, of which waited for: 10 -> 2; matrix products, arithmetic and copies ran while one was open for 4% -> 12% of each run, Pallas kernels for 0% -> 0%
where the time goes in v1:
time: 120 us
  starting transfers between devices  39.4 us (33%)
  local copies, waits for them, and re-layouts  32.9 us (27%)
  other arithmetic  30 us (25%)
  between operations  8.87 us (7%)
  waiting for transfers between devices  8.53 us (7%)
    ppermute x6, starting transfers between devices, exchange(): lax.ppermute(lax.slice_in_dim(array, length - 1, length, axis=dim), axis,...  20 us
    ppermute x6, starting transfers between devices, exchange(): after = lax.ppermute(lax.slice_in_dim(array, 0, 1, axis=dim), axis, down)  14.8 us
    slice x12, local copies, waits for them, and re-layouts, shifted(): inner_up = lax.slice_in_dim(array, 1, length, axis=dim)  11.5 us
    reduce_sum x2, other arithmetic, per_device(): dot = lambda a, b: jnp.sum(a * b)  9.11 us
    mul x1, other arithmetic, per_device(): -0.5 * indexed_values(dilatation, label) * (0.5 + warmth) * stiffness  8.21 us
    slice x9, local copies, waits for them, and re-layouts, shifted(): inner_down = lax.slice_in_dim(array, 0, length - 1, axis=dim)  6.86 us
    all_to_all x1, waiting for transfers between devices, per_device(): rows = lax.all_to_all(jnp.broadcast_to(row[None], (count, 8)), AXES, 0, 0)  4.98 us
    all_to_all x1, starting transfers between devices, per_device(): rows = lax.all_to_all(jnp.broadcast_to(row[None], (count, 8)), AXES, 0, 0)  4.66 us
  transfers between devices with their start and end apart: 13, of which 2 were waited for; matrix products, arithmetic and copies ran while one was open for 12% of the time, Pallas kernels for 0%

profile of v1, /device:TPU:9, one launch (start us, length us, event | category | flops | bytes accessed | tf_op | source)
XLA Modules:
  0.0 119.7 jit_solution(16484875093311194431)
XLA Ops:
  0.6 1.5 %fusion.74 = (f32[1]{0:T(128)}, f32[1]{0:T(128)}, f32[1]{0:T(128)}, f32[1]{0:T(128)}) fusion(f32[4]{0:T(128)} %param.13), kind=kLoop, calls=%fused_computation.162 | loop fusion | bytes 32 | tf_op jit(solution)/shard_map/slice | solution.py:46
  2.1 1.5 %fusion.75 = (f32[1]{0:T(128)}, f32[1]{0:T(128)}, f32[1]{0:T(128)}, f32[1]{0:T(128)}) fusion(f32[4]{0:T(128)} %param.14), kind=kLoop, calls=%fused_computation.163 | loop fusion | bytes 32 | tf_op jit(solution)/shard_map/slice | solution.py:46
  3.6 1.5 %fusion.73 = (f32[1]{0:T(128)}, f32[1]{0:T(128)}, f32[1]{0:T(128)}, f32[1]{0:T(128)}) fusion(f32[4]{0:T(128)} %param.15), kind=kLoop, calls=%fused_computation.161 | loop fusion | bytes 32 | tf_op jit(solution)/shard_map/slice | solution.py:46
  5.0 8.2 %multiply_multiply_fusion = (f32[16,16,512]{2,1,0:T(8,128)}, f32[16,16,512]{2,1,0:T(8,128)S(1)}, pred[16,16,512]{2,1,0:T(8,128)(4,1)S(1)}, pred[16,16,512]{2,1,0...) fusion(f32[16,16,512]{2,1,0:T(8,128)} %param.9, f32[]{:T(128)} %bitcast.26, ...), kind=kLoop, calls=%fused_computation.75 | loop fusion | flops 3932160 | bytes 3670048 | tf_op jit(solution)/shard_map/mul | solution.py:61
  13.2 2.7 %select_add_fusion = f32[16,16,512]{2,1,0:T(8,128)S(1)} fusion(pred[16,16,512]{2,1,0:T(8,128)(4,1)S(1)} %get-tuple-element.27, pred[16,16,512]{2,1,0:T(8,128)(4,1)S(1)} %get-tuple-element.26, pred[16,16,512]{2,1,0:T(8,128)(4,1)S(1)} %get-tuple-element.25, pred[16,16,512]{2,1,0:T(8,128)(4,1)S(1)} %get-tuple-element.24, f32[]{:T(128)} %bitcast.9, f32[]{:T(128)} %bitcast.8, ...), kind=kLoop, calls=%fused_computation.79 | loop fusion | flops 917504 | bytes 1048592 | tf_op jit(solution)/shard_map/add | solution.py:46
  16.3 3.1 %collective-permute-start.3 = (f32[5,16,1,512]{3,2,1,0:T(1,128)S(1)}, f32[5,16,1,512]{3,2,1,0:T(1,128)S(1)}, u32[]{:S(2)}, u32[]{:S(2)}) collective-permute-start(f32[5,16,1,512]{3,2,1,0:T(1,128)S(1)} %get-tuple-element.36), channel_id=1, source_target_pairs={{0,1},{1,2},{2,3},{3,4},{4,5},{5,6},{6,7},{8,9},{9,10},{10,11},{11... | collective-permute-start | bytes 491528 | tf_op jit(solution)/shard_map/ppermute | solution.py:13
  19.4 3.1 %collective-permute-start.2 = (f32[5,16,1,512]{3,2,1,0:T(1,128)S(1)}, f32[5,16,1,512]{3,2,1,0:T(1,128)S(1)}, u32[]{:S(2)}, u32[]{:S(2)}) collective-permute-start(f32[5,16,1,512]{3,2,1,0:T(1,128)S(1)} %get-tuple-element.37), channel_id=1, source_target_pairs={{1,0},{2,1},{3,2},{4,3},{5,4},{6,5},{7,6},{9,8},{10,9},{11,10},{12... | collective-permute-start | bytes 491528 | tf_op jit(solution)/shard_map/ppermute | solution.py:14
  22.5 4.3 %collective-permute-start.1 = (f32[5,1,16,512]{3,2,1,0:T(8,128)S(1)}, f32[5,1,16,512]{3,2,1,0:T(8,128)S(1)}, u32[]{:S(2)}, u32[]{:S(2)}) collective-permute-start(f32[5,1,16,512]{3,2,1,0:T(8,128)S(1)} %get-tuple-element.38), channel_id=1, source_target_pairs={{0,8},{8,16},{16,24},{1,9},{9,17},{17,25},{2,10},{10,18},{18,26},{... | collective-permute-start | bytes 491528 | tf_op jit(solution)/shard_map/ppermute | solution.py:13
  26.8 1.9 %collective-permute-start = (f32[5,1,16,512]{3,2,1,0:T(8,128)S(1)}, f32[5,1,16,512]{3,2,1,0:T(8,128)S(1)}, u32[]{:S(2)}, u32[]{:S(2)}) collective-permute-start(f32[5,1,16,512]{3,2,1,0:T(8,128)S(1)} %get-tuple-element.39), channel_id=1, source_target_pairs={{8,0},{16,8},{24,16},{9,1},{17,9},{25,17},{10,2},{18,10},{26,18},{... | collective-permute-start | bytes 491528 | tf_op jit(solution)/shard_map/ppermute | solution.py:14
  32.8 1.2 fusion.63
  35.0 1.1 fusion.69
  40.5 2.8 %multiply_reduce_fusion.4 = (f32[]{:T(128)}, f32[]{:T(128)}, f32[3,16,16,512]{3,2,1,0:T(8,128)S(1)}) fusion(f32[3,16,16,512]{3,2,1,0:T(8,128)S(1)} %copy-done, f32[3,16,16,511]{3,2,1,0:T(8,128)S(1)} %get-tuple-element.63, f32[16,16,512]{2,1,0:T(8,128)S(1)} %get-tuple-element.35, f32[3,16,16,511]{3,2,1,0:T(8,128)S(1)} %get-tuple-element.62, ...), kind=kLoop, calls=%fused_computation.26 | loop fusion | flops 8257534 | bytes 16246792 | tf_op jit(solution)/shard_map/reduce_sum | solution.py:79
  43.3 2.3 %fusion.52 = (f32[3,16,16,511]{3,2,1,0:T(8,128)}, f32[3,16,16,511]{3,2,1,0:T(8,128)}) fusion(f32[3,16,16,512]{3,2,1,0:T(8,128)S(1)} %get-tuple-element.28), kind=kLoop, calls=%fused_computation.140 | loop fusion | bytes 6279168 | tf_op jit(solution)/shard_map/slice | solution.py:21
  45.6 2.0 %fusion.54 = (f32[3,16,15,512]{3,2,1,0:T(8,128)}, f32[3,16,15,512]{3,2,1,0:T(8,128)}) fusion(f32[3,16,16,512]{3,2,1,0:T(8,128)S(1)} %get-tuple-element.28), kind=kLoop, calls=%fused_computation.142 | loop fusion | bytes 5898240 | tf_op jit(solution)/shard_map/slice | solution.py:22
  47.6 2.0 %fusion.56 = (f32[3,15,16,512]{3,2,1,0:T(8,128)}, f32[3,15,16,512]{3,2,1,0:T(8,128)}) fusion(f32[3,16,16,512]{3,2,1,0:T(8,128)S(1)} %get-tuple-element.28), kind=kLoop, calls=%fused_computation.144 | loop fusion | bytes 5898240 | tf_op jit(solution)/shard_map/slice | solution.py:22
  51.2 1.9 %collective-permute-start.4 = (f32[3,1,16,512]{3,2,1,0:T(8,128)}, f32[3,1,16,512]{3,2,1,0:T(8,128)S(1)}, u32[]{:S(2)}, u32[]{:S(2)}) collective-permute-start(f32[3,1,16,512]{3,2,1,0:T(8,128)} %get-tuple-element.55), channel_id=1, source_target_pairs={{8,0},{16,8},{24,16},{9,1},{17,9},{25,17},{10,2},{18,10},{26,18},{... | collective-permute-start | bytes 294920 | tf_op jit(solution)/shard_map/ppermute | solution.py:14
  53.2 3.6 %collective-permute-start.5 = (f32[3,1,16,512]{3,2,1,0:T(8,128)}, f32[3,1,16,512]{3,2,1,0:T(8,128)S(1)}, u32[]{:S(2)}, u32[]{:S(2)}) collective-permute-start(f32[3,1,16,512]{3,2,1,0:T(8,128)} %get-tuple-element.54), channel_id=1, source_target_pairs={{0,8},{8,16},{16,24},{1,9},{9,17},{17,25},{2,10},{10,18},{18,26},{... | collective-permute-start | bytes 294920 | tf_op jit(solution)/shard_map/ppermute | solution.py:13
  56.8 2.1 %collective-permute-start.6 = (f32[3,16,1,512]{3,2,1,0:T(1,128)}, f32[3,16,1,512]{3,2,1,0:T(1,128)S(1)}, u32[]{:S(2)}, u32[]{:S(2)}) collective-permute-start(f32[3,16,1,512]{3,2,1,0:T(1,128)} %get-tuple-element.51), channel_id=1, source_target_pairs={{1,0},{2,1},{3,2},{4,3},{5,4},{6,5},{7,6},{9,8},{10,9},{11,10},{12... | collective-permute-start | bytes 294920 | tf_op jit(solution)/shard_map/ppermute | solution.py:14
  58.9 3.2 %collective-permute-start.7 = (f32[3,16,1,512]{3,2,1,0:T(1,128)}, f32[3,16,1,512]{3,2,1,0:T(1,128)S(1)}, u32[]{:S(2)}, u32[]{:S(2)}) collective-permute-start(f32[3,16,1,512]{3,2,1,0:T(1,128)} %get-tuple-element.50), channel_id=1, source_target_pairs={{0,1},{1,2},{2,3},{3,4},{4,5},{5,6},{6,7},{8,9},{9,10},{10,11},{11... | collective-permute-start | bytes 294920 | tf_op jit(solution)/shard_map/ppermute | solution.py:13
  63.2 1.2 %fusion.67 = (f32[16,16,511]{2,1,0:T(8,128)}, f32[16,16,511]{2,1,0:T(8,128)}) fusion(f32[16,16,512]{2,1,0:T(8,128)S(1)} %get-tuple-element.43), kind=kLoop, calls=%fused_computation.155 | loop fusion | bytes 2093056 | tf_op jit(solution)/shard_map/slice | solution.py:21
  67.3 6.3 %multiply_reduce_fusion = (f32[]{:T(128)}, f32[]{:T(128)}, f32[]{:T(128)}, f32[]{:T(128)}, f32[]{:T(128)}) fusion(f32[3,16,16,512]{3,2,1,0:T(8,128)S(1)} %copy-done, f32[3,16,16,512]{3,2,1,0:T(8,128)S(1)} %get-tuple-element.28, f32[]{:T(128)} %select_n.53, f32[3,16,16,511]{3,2,1,0:T(8,128)} %get-tuple-element.49, f32[16,16,512]{2,1,0:T(8,128)} %copy-done.9, ...), kind=kLoop, calls=%fused_computation.21 | loop fusion | flops 11403259 | bytes 16246808 | tf_op jit(solution)/shard_map/reduce_sum | solution.py:79
  73.6 4.5 %stack.44 = f32[8]{0:T(128)S(1)} concatenate(f32[1]{0:T(128)} %bitcast, f32[1]{0:T(128)} %bitcast.15, f32[1]{0:T(128)} %bitcast.16, f32[1]{0:T(128)} %bitcast.17, f32[1]{0:T(128)} %bitcast.18, f32[1]{0:T(128)} %bitcast.19, f32[1]{0:T(128)} %bitcast.20, f32[1]{0:T(128)} %bitcast.21), dimensions={0} | concatenate | bytes 64 | tf_op jit(solution)/shard_map/stack | solution.py:83
  78.7 4.7 %all-to-all-start = ((f32[32,1,8]{2,1,0:T(1,128)}), f32[32,1,8]{2,1,0:T(1,128)S(1)}, u32[]{:S(2)}, u32[]{:S(2)}) async-start(f32[32,1,8]{2,1,0:T(1,128)} %broadcast_in_dim.89), calls=%async_computation | async-start | bytes 32768 | tf_op jit(solution)/shard_map/all_to_all | solution.py:85
  84.0 5.0 %all-to-all-done = f32[32,1,8]{2,1,0:T(1,128)S(1)} async-done(((f32[32,1,8]{2,1,0:T(1,128)}), f32[32,1,8]{2,1,0:T(1,128)S(1)}, u32[]{:S(2)}, u32[]{:S(2)}) %all-to-all-start) | async-done | bytes 1056 | tf_op jit(solution)/shard_map/all_to_all | solution.py:85
  96.4 3.9 %multiply_add_fusion.1 = (f32[16,16,512]{2,1,0:T(8,128)S(1)}, f32[16,16,512]{2,1,0:T(8,128)S(1)}, f32[16,16,512]{2,1,0:T(8,128)S(1)}) fusion(f32[]{:T(128)S(6)} %mul.449, f32[]{:T(128)S(6)} %add.249, f32[16,16,512]{2,1,0:T(8,128)} %get-tuple-element.22, f32[16,16,511]{2,1,0:T(8,128)} %get-tuple-element.87, f32[16,16,511]{2,1,0:T(8,128)} %get-tuple-element.86, ...), kind=kLoop, calls=%fused_computation.72 | loop fusion | flops 3014656 | bytes 8384520 | tf_op jit(solution)/shard_map/add | solution.py:110
  100.7 1.5 %multiply_add_fusion = f32[3,16,16,512]{3,2,1,0:T(8,128)} fusion(f32[3,16,16,512]{3,2,1,0:T(8,128)S(1)} %get-tuple-element.28, f32[3,16,16,512]{3,2,1,0:T(8,128)S(1)} %copy-done, f32[]{:T(128)S(6)} %mul.449, f32[]{:T(128)S(6)} %add.249), kind=kLoop, calls=%fused_computation.20 | loop fusion | flops 1179648 | bytes 4718600 | tf_op jit(solution)/shard_map/add | solution.py:98
  102.4 2.4 %collective-permute-start.11 = (f32[2,16,1,512]{3,2,1,0:T(1,128)S(1)}, f32[2,16,1,512]{3,2,1,0:T(1,128)S(1)}, u32[]{:S(2)}, u32[]{:S(2)}) collective-permute-start(f32[2,16,1,512]{3,2,1,0:T(1,128)S(1)} %get-tuple-element.64), channel_id=1, source_target_pairs={{0,1},{1,2},{2,3},{3,4},{4,5},{5,6},{6,7},{8,9},{9,10},{10,11},{11... | collective-permute-start | bytes 196616 | tf_op jit(solution)/shard_map/ppermute | solution.py:13
  104.9 3.9 %collective-permute-start.10 = (f32[2,16,1,512]{3,2,1,0:T(1,128)S(1)}, f32[2,16,1,512]{3,2,1,0:T(1,128)S(1)}, u32[]{:S(2)}, u32[]{:S(2)}) collective-permute-start(f32[2,16,1,512]{3,2,1,0:T(1,128)S(1)} %get-tuple-element.65), channel_id=1, source_target_pairs={{1,0},{2,1},{3,2},{4,3},{5,4},{6,5},{7,6},{9,8},{10,9},{11,10},{12... | collective-permute-start | bytes 196616 | tf_op jit(solution)/shard_map/ppermute | solution.py:14
  108.8 3.3 %collective-permute-start.9 = (f32[2,1,16,512]{3,2,1,0:T(8,128)S(1)}, f32[2,1,16,512]{3,2,1,0:T(8,128)S(1)}, u32[]{:S(2)}, u32[]{:S(2)}) collective-permute-start(f32[2,1,16,512]{3,2,1,0:T(8,128)S(1)} %get-tuple-element.66), channel_id=1, source_target_pairs={{0,8},{8,16},{16,24},{1,9},{9,17},{17,25},{2,10},{10,18},{18,26},{... | collective-permute-start | bytes 196616 | tf_op jit(solution)/shard_map/ppermute | solution.py:13
  112.1 1.9 %collective-permute-start.8 = (f32[2,1,16,512]{3,2,1,0:T(8,128)S(1)}, f32[2,1,16,512]{3,2,1,0:T(8,128)S(1)}, u32[]{:S(2)}, u32[]{:S(2)}) collective-permute-start(f32[2,1,16,512]{3,2,1,0:T(8,128)S(1)} %get-tuple-element.67), channel_id=1, source_target_pairs={{8,0},{16,8},{24,16},{9,1},{17,9},{25,17},{10,2},{18,10},{26,18},{... | collective-permute-start | bytes 196616 | tf_op jit(solution)/shard_map/ppermute | solution.py:14
  114.2 3.5 %collective-permute-done.8 = f32[2,1,16,512]{3,2,1,0:T(8,128)S(1)} collective-permute-done((f32[2,1,16,512]{3,2,1,0:T(8,128)S(1)}, f32[2,1,16,512]{3,2,1,0:T(8,128)S(1)}, u32[]{:S(2)}, u32[]{:S(2)}) %collective-permute-start.8) | collective-permute-done | bytes 65568 | tf_op jit(solution)/shard_map/ppermute | solution.py:14
  117.8 1.9 %fusion.30 = f32[16,16,512]{2,1,0:T(8,128)} fusion(f32[16,16,512]{2,1,0:T(8,128)S(1)} %get-tuple-element.19, f32[16,16,512]{2,1,0:T(8,128)S(1)} %copy-done.2, f32[1,16,512]{2,1,0:T(8,128)S(1)} %copy-done.19, f32[15,16,512]{2,1,0:T(8,128)S(1)} %copy-done.15, f32[1,16,512]{2,1,0:T(8,128)S(1)} %fusion.42, f32[15,16,512]{2,1,0:T(8,128)S(1)} %get-tuple-element.77, ...), kind=kLoop, calls=%fused_computation.58 | loop fusion | flops 5111808 | bytes 7860224 | tf_op jit(solution)/shard_map/add | solution.py:116
  (94 shorter events, 17.0 us)
Async XLA Ops:
  5.0 11.0 %copy-start = (f32[3,16,16,512]{3,2,1,0:T(8,128)S(1)}, f32[3,16,16,512]{3,2,1,0:T(8,128)}, u32[]{:S(2)}) copy-start(f32[3,16,16,512]{3,2,1,0:T(8,128)} %param.8) | copy-start | bytes 4718596
  16.0 20.2 %copy-start.1 = (f32[16,16,512]{2,1,0:T(8,128)}, f32[16,16,512]{2,1,0:T(8,128)S(1)}, u32[]{:S(2)}) copy-start(f32[16,16,512]{2,1,0:T(8,128)S(1)} %select_add_fusion) | copy-start | bytes 1572868
  16.3 20.9 %collective-permute-start.3 = (f32[5,16,1,512]{3,2,1,0:T(1,128)S(1)}, f32[5,16,1,512]{3,2,1,0:T(1,128)S(1)}, u32[]{:S(2)}, u32[]{:S(2)}) collective-permute-start(f32[5,16,1,512]{3,2,1,0:T(1,128)S(1)} %get-tuple-element.36), channel_id=1, source_target_pairs={{0,1},{1,2},{2,3},{3,4},{4,5},{5,6},{6,7},{8,9},{9,10},{10,11},{11... | collective-permute-start | bytes 491528 | tf_op jit(solution)/shard_map/ppermute | solution.py:13
  19.4 18.4 %collective-permute-start.2 = (f32[5,16,1,512]{3,2,1,0:T(1,128)S(1)}, f32[5,16,1,512]{3,2,1,0:T(1,128)S(1)}, u32[]{:S(2)}, u32[]{:S(2)}) collective-permute-start(f32[5,16,1,512]{3,2,1,0:T(1,128)S(1)} %get-tuple-element.37), channel_id=1, source_target_pairs={{1,0},{2,1},{3,2},{4,3},{5,4},{6,5},{7,6},{9,8},{10,9},{11,10},{12... | collective-permute-start | bytes 491528 | tf_op jit(solution)/shard_map/ppermute | solution.py:14
  22.5 16.0 %collective-permute-start.1 = (f32[5,1,16,512]{3,2,1,0:T(8,128)S(1)}, f32[5,1,16,512]{3,2,1,0:T(8,128)S(1)}, u32[]{:S(2)}, u32[]{:S(2)}) collective-permute-start(f32[5,1,16,512]{3,2,1,0:T(8,128)S(1)} %get-tuple-element.38), channel_id=1, source_target_pairs={{0,8},{8,16},{16,24},{1,9},{9,17},{17,25},{2,10},{10,18},{18,26},{... | collective-permute-start | bytes 491528 | tf_op jit(solution)/shard_map/ppermute | solution.py:13
  26.8 12.3 %collective-permute-start = (f32[5,1,16,512]{3,2,1,0:T(8,128)S(1)}, f32[5,1,16,512]{3,2,1,0:T(8,128)S(1)}, u32[]{:S(2)}, u32[]{:S(2)}) collective-permute-start(f32[5,1,16,512]{3,2,1,0:T(8,128)S(1)} %get-tuple-element.39), channel_id=1, source_target_pairs={{8,0},{16,8},{24,16},{9,1},{17,9},{25,17},{10,2},{18,10},{26,18},{... | collective-permute-start | bytes 491528 | tf_op jit(solution)/shard_map/ppermute | solution.py:14
  40.4 2.9 %copy-start.3 = (f32[16,16,512]{2,1,0:T(8,128)}, f32[16,16,512]{2,1,0:T(8,128)S(1)}, u32[]{:S(2)}) copy-start(f32[16,16,512]{2,1,0:T(8,128)S(1)} %get-tuple-element.29) | copy-start | bytes 1572868
  40.4 2.9 %copy-start.4 = (f32[16,16,512]{2,1,0:T(8,128)}, f32[16,16,512]{2,1,0:T(8,128)S(1)}, u32[]{:S(2)}) copy-start(f32[16,16,512]{2,1,0:T(8,128)S(1)} %get-tuple-element.30) | copy-start | bytes 1572868
  40.4 2.9 %copy-start.5 = (f32[16,16,512]{2,1,0:T(8,128)}, f32[16,16,512]{2,1,0:T(8,128)S(1)}, u32[]{:S(2)}) copy-start(f32[16,16,512]{2,1,0:T(8,128)S(1)} %get-tuple-element.31) | copy-start | bytes 1572868
  40.4 2.9 %copy-start.6 = (f32[16,16,512]{2,1,0:T(8,128)}, f32[16,16,512]{2,1,0:T(8,128)S(1)}, u32[]{:S(2)}) copy-start(f32[16,16,512]{2,1,0:T(8,128)S(1)} %get-tuple-element.32) | copy-start | bytes 1572868
  40.4 2.9 %copy-start.7 = (f32[16,16,512]{2,1,0:T(8,128)}, f32[16,16,512]{2,1,0:T(8,128)S(1)}, u32[]{:S(2)}) copy-start(f32[16,16,512]{2,1,0:T(8,128)S(1)} %get-tuple-element.33) | copy-start | bytes 1572868
  40.4 2.9 %copy-start.8 = (f32[16,16,512]{2,1,0:T(8,128)}, f32[16,16,512]{2,1,0:T(8,128)S(1)}, u32[]{:S(2)}) copy-start(f32[16,16,512]{2,1,0:T(8,128)S(1)} %get-tuple-element.34) | copy-start | bytes 1572868
  51.2 16.0 %collective-permute-start.4 = (f32[3,1,16,512]{3,2,1,0:T(8,128)}, f32[3,1,16,512]{3,2,1,0:T(8,128)S(1)}, u32[]{:S(2)}, u32[]{:S(2)}) collective-permute-start(f32[3,1,16,512]{3,2,1,0:T(8,128)} %get-tuple-element.55), channel_id=1, source_target_pairs={{8,0},{16,8},{24,16},{9,1},{17,9},{25,17},{10,2},{18,10},{26,18},{... | collective-permute-start | bytes 294920 | tf_op jit(solution)/shard_map/ppermute | solution.py:14
  53.2 14.1 %collective-permute-start.5 = (f32[3,1,16,512]{3,2,1,0:T(8,128)}, f32[3,1,16,512]{3,2,1,0:T(8,128)S(1)}, u32[]{:S(2)}, u32[]{:S(2)}) collective-permute-start(f32[3,1,16,512]{3,2,1,0:T(8,128)} %get-tuple-element.54), channel_id=1, source_target_pairs={{0,8},{8,16},{16,24},{1,9},{9,17},{17,25},{2,10},{10,18},{18,26},{... | collective-permute-start | bytes 294920 | tf_op jit(solution)/shard_map/ppermute | solution.py:13
  56.8 10.5 %collective-permute-start.6 = (f32[3,16,1,512]{3,2,1,0:T(1,128)}, f32[3,16,1,512]{3,2,1,0:T(1,128)S(1)}, u32[]{:S(2)}, u32[]{:S(2)}) collective-permute-start(f32[3,16,1,512]{3,2,1,0:T(1,128)} %get-tuple-element.51), channel_id=1, source_target_pairs={{1,0},{2,1},{3,2},{4,3},{5,4},{6,5},{7,6},{9,8},{10,9},{11,10},{12... | collective-permute-start | bytes 294920 | tf_op jit(solution)/shard_map/ppermute | solution.py:14
  58.9 8.4 %collective-permute-start.7 = (f32[3,16,1,512]{3,2,1,0:T(1,128)}, f32[3,16,1,512]{3,2,1,0:T(1,128)S(1)}, u32[]{:S(2)}, u32[]{:S(2)}) collective-permute-start(f32[3,16,1,512]{3,2,1,0:T(1,128)} %get-tuple-element.50), channel_id=1, source_target_pairs={{0,1},{1,2},{2,3},{3,4},{4,5},{5,6},{6,7},{8,9},{9,10},{10,11},{11... | collective-permute-start | bytes 294920 | tf_op jit(solution)/shard_map/ppermute | solution.py:13
  78.7 10.3 %all-to-all-start = ((f32[32,1,8]{2,1,0:T(1,128)}), f32[32,1,8]{2,1,0:T(1,128)S(1)}, u32[]{:S(2)}, u32[]{:S(2)}) async-start(f32[32,1,8]{2,1,0:T(1,128)} %broadcast_in_dim.89), calls=%async_computation | async-start | bytes 32768 | tf_op jit(solution)/shard_map/all_to_all | solution.py:85
  100.7 17.0 %copy-start.14 = (f32[15,16,512]{2,1,0:T(8,128)S(1)}, f32[15,16,512]{2,1,0:T(8,128)}, u32[]{:S(2)}) copy-start(f32[15,16,512]{2,1,0:T(8,128)} %get-tuple-element.78) | copy-start | bytes 1474564
  100.7 17.0 %copy-start.15 = (f32[15,16,512]{2,1,0:T(8,128)S(1)}, f32[15,16,512]{2,1,0:T(8,128)}, u32[]{:S(2)}) copy-start(f32[15,16,512]{2,1,0:T(8,128)} %get-tuple-element.79) | copy-start | bytes 1474564
  102.2 15.5 %copy-start.2 = (f32[16,16,512]{2,1,0:T(8,128)S(1)}, f32[16,16,512]{2,1,0:T(8,128)}, u32[]{:S(2)}) copy-start(f32[16,16,512]{2,1,0:T(8,128)} %copy-done.1) | copy-start | bytes 1572868
  102.3 15.5 %copy-start.10 = (f32[16,16,511]{2,1,0:T(8,128)S(1)}, f32[16,16,511]{2,1,0:T(8,128)}, u32[]{:S(2)}) copy-start(f32[16,16,511]{2,1,0:T(8,128)} %get-tuple-element.68) | copy-start | bytes 1569796
  102.3 15.5 %copy-start.11 = (f32[16,16,511]{2,1,0:T(8,128)S(1)}, f32[16,16,511]{2,1,0:T(8,128)}, u32[]{:S(2)}) copy-start(f32[16,16,511]{2,1,0:T(8,128)} %get-tuple-element.69) | copy-start | bytes 1569796
  102.3 15.5 %copy-start.12 = (f32[16,15,512]{2,1,0:T(8,128)S(1)}, f32[16,15,512]{2,1,0:T(8,128)}, u32[]{:S(2)}) copy-start(f32[16,15,512]{2,1,0:T(8,128)} %get-tuple-element.74) | copy-start | bytes 1474564
  102.3 15.5 %copy-start.13 = (f32[16,15,512]{2,1,0:T(8,128)S(1)}, f32[16,15,512]{2,1,0:T(8,128)}, u32[]{:S(2)}) copy-start(f32[16,15,512]{2,1,0:T(8,128)} %get-tuple-element.75) | copy-start | bytes 1474564
  102.3 15.5 %copy-start.16 = (f32[16,1,512]{2,1,0:T(1,128)S(1)}, f32[16,1,512]{2,1,0:T(1,128)}, u32[]{:S(2)}) copy-start(f32[16,1,512]{2,1,0:T(1,128)} %get-tuple-element.94) | copy-start | bytes 98308
  102.3 15.5 %copy-start.17 = (f32[16,1,512]{2,1,0:T(1,128)S(1)}, f32[16,1,512]{2,1,0:T(1,128)}, u32[]{:S(2)}) copy-start(f32[16,1,512]{2,1,0:T(1,128)} %get-tuple-element.97) | copy-start | bytes 98308
  102.3 15.5 %copy-start.18 = (f32[1,16,512]{2,1,0:T(8,128)S(1)}, f32[1,16,512]{2,1,0:T(8,128)}, u32[]{:S(2)}) copy-start(f32[1,16,512]{2,1,0:T(8,128)} %get-tuple-element.100) | copy-start | bytes 98308
  102.3 15.5 %copy-start.19 = (f32[1,16,512]{2,1,0:T(8,128)S(1)}, f32[1,16,512]{2,1,0:T(8,128)}, u32[]{:S(2)}) copy-start(f32[1,16,512]{2,1,0:T(8,128)} %get-tuple-element.103) | copy-start | bytes 98308
  102.4 11.6 %collective-permute-start.11 = (f32[2,16,1,512]{3,2,1,0:T(1,128)S(1)}, f32[2,16,1,512]{3,2,1,0:T(1,128)S(1)}, u32[]{:S(2)}, u32[]{:S(2)}) collective-permute-start(f32[2,16,1,512]{3,2,1,0:T(1,128)S(1)} %get-tuple-element.64), channel_id=1, source_target_pairs={{0,1},{1,2},{2,3},{3,4},{4,5},{5,6},{6,7},{8,9},{9,10},{10,11},{11... | collective-permute-start | bytes 196616 | tf_op jit(solution)/shard_map/ppermute | solution.py:13
  104.9 9.3 %collective-permute-start.10 = (f32[2,16,1,512]{3,2,1,0:T(1,128)S(1)}, f32[2,16,1,512]{3,2,1,0:T(1,128)S(1)}, u32[]{:S(2)}, u32[]{:S(2)}) collective-permute-start(f32[2,16,1,512]{3,2,1,0:T(1,128)S(1)} %get-tuple-element.65), channel_id=1, source_target_pairs={{1,0},{2,1},{3,2},{4,3},{5,4},{6,5},{7,6},{9,8},{10,9},{11,10},{12... | collective-permute-start | bytes 196616 | tf_op jit(solution)/shard_map/ppermute | solution.py:14
  108.8 5.4 %collective-permute-start.9 = (f32[2,1,16,512]{3,2,1,0:T(8,128)S(1)}, f32[2,1,16,512]{3,2,1,0:T(8,128)S(1)}, u32[]{:S(2)}, u32[]{:S(2)}) collective-permute-start(f32[2,1,16,512]{3,2,1,0:T(8,128)S(1)} %get-tuple-element.66), channel_id=1, source_target_pairs={{0,8},{8,16},{16,24},{1,9},{9,17},{17,25},{2,10},{10,18},{18,26},{... | collective-permute-start | bytes 196616 | tf_op jit(solution)/shard_map/ppermute | solution.py:13
  112.1 5.6 %collective-permute-start.8 = (f32[2,1,16,512]{3,2,1,0:T(8,128)S(1)}, f32[2,1,16,512]{3,2,1,0:T(8,128)S(1)}, u32[]{:S(2)}, u32[]{:S(2)}) collective-permute-start(f32[2,1,16,512]{3,2,1,0:T(8,128)S(1)} %get-tuple-element.67), channel_id=1, source_target_pairs={{8,0},{16,8},{24,16},{9,1},{17,9},{25,17},{10,2},{18,10},{26,18},{... | collective-permute-start | bytes 196616 | tf_op jit(solution)/shard_map/ppermute | solution.py:14
  (1 other events, 2.9 us)

commit v2 on v1

v2 whole, which is shorter than its diff:
```python
import functools

import jax
import jax.numpy as jnp
from jax import lax
from jax.experimental import pallas as pl
from jax.experimental.pallas import tpu as pltpu
from jax.sharding import PartitionSpec as P

AXES = ("gx", "gy")
INTERPRET = False
F32 = jnp.float32
VMEM = pl.BlockSpec(memory_space=pltpu.VMEM)
SMEM = pl.BlockSpec(memory_space=pltpu.SMEM)

SIDE = 10
CORNER_ROWS = 24


def call(kernel, out_shape, in_specs, out_specs=None, **extra):
    out_specs = jax.tree.map(lambda _: VMEM, out_shape) if out_specs is None else out_specs
    return pl.pallas_call(
        kernel, out_shape=out_shape, in_specs=in_specs, out_specs=out_specs, interpret=INTERPRET, **extra
    )


def shape(*dims):
    return jax.ShapeDtypeStruct(dims, F32)


def z_pair(value):
    length = value.shape[-1]
    lane = lax.broadcasted_iota(jnp.int32, value.shape, value.ndim - 1)
    after = jnp.where(lane == length - 1, 0.0, pltpu.roll(value, length - 1, value.ndim - 1))
    before = jnp.where(lane == 0, 0.0, pltpu.roll(value, 1, value.ndim - 1))
    return after, before


def row_pair(value, row_before, row_after):
    length = value.shape[0]
    row = lax.broadcasted_iota(jnp.int32, value.shape, 0)
    after = jnp.where(row == length - 1, row_after, pltpu.roll(value, length - 1, 0))
    before = jnp.where(row == 0, row_before, pltpu.roll(value, 1, 0))
    return after, before


def apply(center, lead_before, lead_after, row_before, row_after):
    near = [
        (a, b) + row_pair(c, p, n) + z_pair(c)
        for c, b, a, p, n in zip(center, lead_before, lead_after, row_before, row_after)
    ]
    weights = [center[0] + other for other in near[0]]
    diagonal = 0.5 + sum(weights)
    out = []
    for value, others in zip(center[1:], near[1:]):
        total = diagonal * value
        for weight, other in zip(weights, others):
            total = total - weight * other
        out.append(total)
    return out


def lookup(label, table):
    count = table.shape[0]
    value = jnp.full(label.shape, table[count - 1], F32)
    for index in range(count - 1):
        value = jnp.where(label == index, table[index], value)
    return value


def prepare_kernel(
    rigidity, dilatation, diffusivity, motion, warmth, yielding, printed, label,
    half, kappa, links, y_down, y_up, late_down, late_up, x_down, x_up,
):
    depth_x, rows = half.shape[0], half.shape[1]
    for x in range(depth_x):
        kind = label[x]
        h = (
            0.5 * lookup(kind, rigidity)
            * (1.0 - 0.7 * yielding[x].astype(F32))
            * (0.05 + 0.95 * printed[x].astype(F32))
        )
        half[x] = h
        kappa[x] = -lookup(kind, dilatation) * (0.5 + warmth[x]) * h
        links[x] = 0.075 * lookup(kind, diffusivity)
    for x in range(depth_x):
        for out, late, order in ((y_down, late_down, (0, 1, 2)), (y_up, late_up, (rows - 1, rows - 2, rows - 3))):
            for depth in range(2):
                at = pl.ds(order[depth], 1)
                for c in range(3):
                    out[4 * depth + c, pl.ds(x, 1), :] = motion[c, x, at, :]
                out[4 * depth + 3, pl.ds(x, 1), :] = half[x, at, :]
            late[0, pl.ds(x, 1), :] = motion[1, x, pl.ds(order[2], 1), :]
            late[1, pl.ds(x, 1), :] = half[x, pl.ds(order[2], 1), :]
            late[2, pl.ds(x, 1), :] = kappa[x, pl.ds(order[0], 1), :]
            late[3, pl.ds(x, 1), :] = links[x, pl.ds(order[0], 1), :]

    def planes(out, order):
        for depth in range(2):
            for c in range(3):
                out[4 * depth + c] = motion[c, order[depth]]
            out[4 * depth + 3] = half[order[depth]]
        out[8] = motion[0, order[2]]
        out[9] = half[order[2]]
        out[10] = kappa[order[0]]
        out[11] = links[order[0]]

    @pl.when(pl.program_id(0) == 0)
    def _():
        planes(x_down, (0, 1, 2))

    @pl.when(pl.program_id(0) == pl.num_programs(0) - 1)
    def _():
        planes(x_up, (depth_x - 1, depth_x - 2, depth_x - 3))


def prepare(motion, warmth, yielding, printed, label, rigidity, dilatation, diffusivity):
    _, nx, ny, nz = motion.shape
    block = 8
    field = pl.BlockSpec((block, ny, nz), lambda i: (i, 0, 0))
    rows = lambda n: pl.BlockSpec((n, block, nz), lambda i: (0, i, 0))
    whole = pl.BlockSpec((12, ny, nz), lambda i: (0, 0, 0))
    return call(
        prepare_kernel,
        (shape(nx, ny, nz),) * 3
        + (shape(8, nx, nz),) * 2 + (shape(4, nx, nz),) * 2 + (shape(12, ny, nz),) * 2,
        [SMEM] * 3 + [pl.BlockSpec((3, block, ny, nz), lambda i: (0, i, 0, 0))] + [field] * 4,
        (field,) * 3 + (rows(8),) * 2 + (rows(4),) * 2 + (whole,) * 2,
        grid=(nx // block,),
    )(rigidity, dilatation, diffusivity, motion, warmth, yielding, printed, label)


def corner_kernel(x_low, x_high, down, up):
    rows = x_low.shape[1]
    for side, planes in ((0, x_low), (SIDE, x_high)):
        for out, near, far in ((down, 0, 1), (up, rows - 1, rows - 2)):
            for k, plane in enumerate((0, 1, 2, 3, 4, 5, 7)):
                out[pl.ds(side + k, 1), :] = planes[plane, pl.ds(near, 1), :]
            for k, plane in enumerate((0, 1, 3)):
                out[pl.ds(side + 7 + k, 1), :] = planes[plane, pl.ds(far, 1), :]
    for out in (down, up):
        out[pl.ds(2 * SIDE, CORNER_ROWS - 2 * SIDE), :] = jnp.zeros((CORNER_ROWS - 2 * SIDE, out.shape[1]), F32)


def corners(x_low, x_high):
    _, ny, nz = x_low.shape
    return call(
        corner_kernel, (shape(CORNER_ROWS, nz),) * 2,
        [pl.BlockSpec((8, ny, nz), lambda i: (0, 0, 0))] * 2,
        (pl.BlockSpec((CORNER_ROWS, nz), lambda i: (0, 0)),) * 2, grid=(1,),
    )(x_low, x_high)


def fold(value):
    rows, length = value.shape
    value = sum(value[8 * k : 8 * k + 8] for k in range(rows // 8))
    return sum(value[:, 128 * k : 128 * k + 128] for k in range(length // 128))


def total(value):
    return jnp.sum(jnp.sum(value, axis=1, keepdims=True), axis=0, keepdims=True)


def over(planes, body, carry):
    carry = body(0, True, False, carry)
    carry = lax.fori_loop(1, planes - 1, lambda x, c: body(x, False, False, c), carry)
    return body(planes - 1, False, True, carry)


def sums_kernel(
    motion, half, x_low, x_high, y_low, y_high, c_low, c_high, own_low, own_high, q, qx, qy, rows_out
):
    nx, ny, nz = half.shape
    row = lambda ref, k: ref[pl.ds(k, 1), :]
    planes = lambda ref, base: [ref[base + 3], ref[base], ref[base + 1], ref[base + 2]]
    lines = lambda ref, base: [row(ref, base + k) for k in (3, 0, 1, 2)]
    own = lambda x: [half[x], motion[0, x], motion[1, x], motion[2, x]]
    beyond = lambda ref, x: [ref[k, pl.ds(x, 1), :] for k in (3, 0, 1, 2)]

    def store(out, base, center, values):
        for c, value in enumerate(values):
            out[base + c] = jnp.where(center[0] > 0.0, value, 0.0)

    near = planes(x_low, 0)
    store(qx, 0, near, apply(near, planes(x_low, 4), own(0), lines(c_low, 0), lines(c_high, 0)))
    near = planes(x_high, 0)
    store(qx, 3, near, apply(near, own(nx - 1), planes(x_high, 4), lines(c_low, SIDE), lines(c_high, SIDE)))
    near = planes(y_low, 0)
    store(qy, 0, near, apply(near, planes(y_low, 4), planes(own_low, 0), lines(c_low, 0), lines(c_low, SIDE)))
    near = planes(y_high, 0)
    store(qy, 3, near, apply(near, planes(own_high, 0), planes(y_high, 4), lines(c_high, 0), lines(c_high, SIDE)))

    def first(x, is_first, is_last, carry):
        rr, rq, qq = carry
        center = own(x)
        before = planes(x_low, 0) if is_first else own(x - 1)
        after = planes(x_high, 0) if is_last else own(x + 1)
        values = apply(center, before, after, beyond(y_low, x), beyond(y_high, x))
        for c, (r, value) in enumerate(zip(center[1:], values)):
            q[c, x] = value
            rr, rq, qq = rr + fold(r * r), rq + fold(r * value), qq + fold(value * value)
        return rr, rq, qq

    zero = jnp.zeros((8, 128), F32)
    rr, rq, qq = map(total, over(nx, first, (zero,) * 3))
    shift = jnp.where(qq > 0.0, rq / jnp.where(qq > 0.0, qq, 1.0), 0.0)

    def second(x, is_first, is_last, carry):
        uu, uq, uz, qz = carry
        values = lambda ref, at: [ref[at(c)] for c in range(3)]
        center = [half[x]] + [q[c, x] for c in range(3)]
        before = [x_low[3]] + [qx[c] for c in range(3)] if is_first else [half[x - 1]] + [q[c, x - 1] for c in range(3)]
        after = [x_high[3]] + [qx[3 + c] for c in range(3)] if is_last else [half[x + 1]] + [q[c, x + 1] for c in range(3)]
        low = [y_low[3, pl.ds(x, 1), :]] + [qy[c, pl.ds(x, 1), :] for c in range(3)]
        high = [y_high[3, pl.ds(x, 1), :]] + [qy[3 + c, pl.ds(x, 1), :] for c in range(3)]
        for c, z in enumerate(apply(center, before, after, low, high)):
            u = motion[c, x] - shift * center[1 + c]
            uu, uq = uu + fold(u * u), uq + fold(u * center[1 + c])
            uz, qz = uz + fold(u * z), qz + fold(center[1 + c] * z)
        return uu, uq, uz, qz

    uu, uq, uz, qz = map(total, over(nx, second, (zero,) * 4))
    lane = lax.broadcasted_iota(jnp.int32, (1, 128), 1)
    line = jnp.zeros((1, 128), F32)
    for k, value in enumerate((rr, rq, qq, qz, shift, uu, uq, uz)):
        line = jnp.where(lane == k, value, line)
    rows_out[...] = jnp.broadcast_to(line, rows_out.shape)


def late_kernel(
    x_low, x_high, y_low, y_high, late_low, late_high, c_low, c_high, q_x, q_y, q_corner,
):
    row = lambda ref, k: ref[pl.ds(k, 1), :]
    masked = lambda h, value: jnp.where(h > 0.0, value, 0.0)
    ny, nx = x_low.shape[1], y_low.shape[1]

    def one(center, before, after, low, high):
        return masked(center[0], apply(center, before, after, low, high)[0])

    p = lambda ref, *ks: [ref[k] for k in ks]
    r = lambda ref, *ks: [row(ref, k) for k in ks]
    q_x[0] = one(p(x_low, 7, 4), p(x_low, 9, 8), p(x_low, 3, 0), r(c_low, 6, 4), r(c_high, 6, 4))
    q_x[1] = one(p(x_high, 7, 4), p(x_high, 3, 0), p(x_high, 9, 8), r(c_low, SIDE + 6, SIDE + 4), r(c_high, SIDE + 6, SIDE + 4))
    q_y[0] = one(p(y_low, 7, 5), p(late_low, 1, 0), p(y_low, 3, 1), r(c_low, 9, 8), r(c_low, SIDE + 9, SIDE + 8))
    q_y[1] = one(p(y_high, 7, 5), p(y_high, 3, 1), p(late_high, 1, 0), r(c_high, 9, 8), r(c_high, SIDE + 9, SIDE + 8))
    q_corner[...] = jnp.zeros(q_corner.shape, F32)
    for k, (c, base, x, y, px, py) in enumerate((
        (c_low, 0, 0, 0, x_low, y_low),
        (c_low, SIDE, nx - 1, 0, x_high, y_low),
        (c_high, 0, 0, ny - 1, x_low, y_high),
        (c_high, SIDE, nx - 1, ny - 1, x_high, y_high),
    )):
        h = row(c, base + 3)
        beside = lambda plane, out_x, out_y: [
            row(c, base + out_x), row(c, base + out_y), py[plane, pl.ds(x, 1), :], px[plane, pl.ds(y, 1), :]
        ]
        h_near = beside(3, 6, 9)
        for comp in range(2):
            value = row(c, base + comp)
            acc = 0.5 * value
            for hn, vn in zip(h_near + list(z_pair(h)), beside(comp, 4 + comp, 7 + comp) + list(z_pair(value))):
                acc = acc + (h + hn) * (value - vn)
            q_corner[pl.ds(4 * comp + k, 1), :] = masked(h, acc)


def finish_kernel(
    rows, motion, q, kappa, links, x_low, x_high, y_low, y_high, late_low, late_high, c_low, c_high,
    qx, qy, q_x, q_y, q_corner, solution, thermal, source, source_low, source_high, edge,
):
    nx, ny, nz = kappa.shape
    table = rows[...]
    column = lambda k: table[:, k : k + 1]
    summed = lambda value: jnp.sum(value, axis=0, keepdims=True)
    rr, rq, qq, qz, shift, uu, uq, uz = [column(k) for k in range(8)]
    total_rr = summed(rr)
    step = total_rr / summed(rq)
    gap = step - shift
    next_rr = summed(uu - 2.0 * gap * uq + gap * gap * qq)
    energy = summed((uq - shift * uz) - gap * (uz + qq - shift * qz) + gap * gap * qz)
    ratio = next_rr / total_rr
    next_step = next_rr / (energy - ratio * next_rr / step)
    c0 = step + next_step * (1.0 + ratio)
    c1 = -next_step * step
    mix = lambda a, b: c0 * a + c1 * b
    row = lambda ref, k: ref[pl.ds(k, 1), :]

    def z_diff(value):
        after, before = z_pair(value)
        return after - before

    def row_diff(value, row_before, row_after):
        after, before = row_pair(value, row_before, row_after)
        return after - before

    def combine(x, carry):
        for c in range(3):
            solution[c, x] = mix(motion[c, x], q[c, x])
        edge[0, pl.ds(x, 1), :] = solution[1, x, pl.ds(0, 1), :]
        edge[1, pl.ds(x, 1), :] = solution[1, x, pl.ds(ny - 1, 1), :]
        return carry

    for x in range(nx):
        combine(x, 0)
    corner = lambda c_ref, base, comp, k: mix(row(c_ref, base + comp), row(q_corner, 4 * comp + k))
    x_of = lambda planes, base, c: mix(planes[c], qx[base + c])
    y_of = lambda planes, base, c: mix(planes[c], qy[base + c])
    s_x_low = x_low[10] * (
        solution[0, 0] - mix(x_low[4], q_x[0])
        + row_diff(x_of(x_low, 0, 1), corner(c_low, 0, 1, 0), corner(c_high, 0, 1, 2))
        + z_diff(x_of(x_low, 0, 2))
    )
    s_x_high = x_high[10] * (
        mix(x_high[4], q_x[1]) - solution[0, nx - 1]
        + row_diff(x_of(x_high, 3, 1), corner(c_low, SIDE, 1, 1), corner(c_high, SIDE, 1, 3))
        + z_diff(x_of(x_high, 3, 2))
    )
    source_low[...] = late_low[2] * (
        row_diff(y_of(y_low, 0, 0), corner(c_low, 0, 0, 0), corner(c_low, SIDE, 0, 1))
        + edge[0] - mix(y_low[5], q_y[0]) + z_diff(y_of(y_low, 0, 2))
    )
    source_high[...] = late_high[2] * (
        row_diff(y_of(y_high, 3, 0), corner(c_high, 0, 0, 2), corner(c_high, SIDE, 0, 3))
        + mix(y_high[5], q_y[1]) - edge[1] + z_diff(y_of(y_high, 3, 2))
    )

    def first(x, is_first, is_last, carry):
        before = x_of(x_low, 0, 0) if is_first else solution[0, x - 1]
        after = x_of(x_high, 3, 0) if is_last else solution[0, x + 1]
        low = mix(y_low[1, pl.ds(x, 1), :], qy[1, pl.ds(x, 1), :])
        high = mix(y_high[1, pl.ds(x, 1), :], qy[4, pl.ds(x, 1), :])
        source[x] = kappa[x] * (after - before + row_diff(solution[1, x], low, high) + z_diff(solution[2, x]))
        return carry

    over(nx, first, 0)

    def second(x, is_first, is_last, carry):
        s, g = source[x], links[x]
        s_before, g_before = (s_x_low, x_low[11]) if is_first else (source[x - 1], links[x - 1])
        s_after, g_after = (s_x_high, x_high[11]) if is_last else (source[x + 1], links[x + 1])
        at = pl.ds(x, 1)
        s_near = (s_before, s_after) + row_pair(s, source_low[at, :], source_high[at, :]) + z_pair(s)
        g_near = (g_before, g_after) + row_pair(g, late_low[3, at, :], late_high[3, at, :]) + z_pair(g)
        value = s
        for sn, gn in zip(s_near, g_near):
            value = value + (g + gn) * (sn - s)
        thermal[x] = value
        return carry

    over(nx, second, 0)


def per_device(motion, warmth, yielding, printed, label, rigidity, dilatation, diffusivity):
    _, nx, ny, nz = motion.shape
    devices = lax.axis_size(AXES)

    def swap(axis, down, up):
        count = lax.axis_size(axis)
        high = lax.ppermute(down, axis, [(i + 1, i) for i in range(count - 1)])
        low = lax.ppermute(up, axis, [(i, i + 1) for i in range(count - 1)])
        return low, high

    half, kappa, links, y_down, y_up, late_down, late_up, x_down, x_up = prepare(
        motion, warmth, yielding, printed, label, rigidity, dilatation, diffusivity
    )
    x_low, x_high = swap("gx", x_down, x_up)
    y_low, y_high = swap("gy", y_down, y_up)
    c_low, c_high = swap("gy", *corners(x_low, x_high))
    late_low, late_high = swap("gy", late_down, late_up)
    q, qx, qy, rows = call(
        sums_kernel,
        (shape(3, nx, ny, nz), shape(6, ny, nz), shape(6, nx, nz), shape(devices, 128)),
        [VMEM] * 10,
    )(motion, half, x_low, x_high, y_low, y_high, c_low, c_high, y_down, y_up)
    rows = lax.all_to_all(rows, AXES, 0, 0, tiled=True)
    q_x, q_y, q_corner = call(
        late_kernel, (shape(2, ny, nz), shape(2, nx, nz), shape(8, nz)), [VMEM] * 8
    )(x_low, x_high, y_low, y_high, late_low, late_high, c_low, c_high)
    return call(
        finish_kernel,
        (shape(3, nx, ny, nz), shape(nx, ny, nz)),
        [VMEM] * 18,
        scratch_shapes=[
            pltpu.VMEM((nx, ny, nz), F32), pltpu.VMEM((nx, nz), F32),
            pltpu.VMEM((nx, nz), F32), pltpu.VMEM((2, nx, nz), F32),
        ],
    )(
        rows, motion, q, kappa, links, x_low, x_high, y_low, y_high, late_low, late_high, c_low, c_high,
        qx, qy, q_x, q_y, q_corner,
    )


def solution(mesh):
    field = P("gx", "gy", None)
    in_specs = (P(None, "gx", "gy", None), field, field, field, field, P(), P(), P())
    out_specs = (P(None, "gx", "gy", None), field)
    return jax.shard_map(
        per_device, mesh=mesh, in_specs=in_specs, out_specs=out_specs, check_vma=False
    )
```

time: 120 us -> 67.8 us (0.56)
  the two profiles are of different devices: /device:TPU:9 before, /device:TPU:0 now
where the time goes in v2:
time: 67.8 us; the launch traced here: 67.4 us
  starting transfers between devices  30.1 us (44%)
  Pallas kernels  23.9 us (35%)
  waiting for transfers between devices  9.27 us (14%)
  local copies, waits for them, and re-layouts  3.25 us (5%)
  between operations  0.82 us (1%)
    ppermute x4, starting transfers between devices, swap(): low = lax.ppermute(up, axis, [(i, i + 1) for i in range(count - 1)])  16.2 us
    all_to_all x1, starting transfers between devices, per_device(): rows = lax.all_to_all(rows, AXES, 0, 0, tiled=True)  8.77 us
    pallas_call x1, Pallas kernels, per_device(): call(sums_kernel, (shape(3, nx, ny, nz), shape(6, ny, nz), shape(6, nx, n...  8.42 us
    pallas_call x1, Pallas kernels, per_device(): call(finish_kernel, (shape(3, nx, ny, nz), shape(nx, ny, nz)), [VMEM] * 1...  7.81 us
    ppermute x4, starting transfers between devices, swap(): high = lax.ppermute(down, axis, [(i + 1, i) for i in range(count - 1)])  5.17 us
    pallas_call x1, Pallas kernels, prepare(): call(prepare_kernel, (shape(nx, ny, nz),) * 3 + (shape(8, nx, nz),) * 2 +...  3.76 us
    ppermute x4, waiting for transfers between devices, swap(): high = lax.ppermute(down, axis, [(i + 1, i) for i in range(count - 1)])  3.61 us
    all_to_all x1, waiting for transfers between devices, per_device(): rows = lax.all_to_all(rows, AXES, 0, 0, tiled=True)  3.48 us
  transfers between devices with their start and end apart: 9, of which 3 were waited for; matrix products, arithmetic and copies ran while one was open for 0% of the time, Pallas kernels for 18%

profile of v2, /device:TPU:0, one launch (start us, length us, event | category | flops | bytes accessed | tf_op | source)
XLA Modules:
  0.0 67.4 jit_solution(14640174525113222820)
XLA Ops:
  0.6 3.8 %shard_map.95 = (f32[16,16,512]{2,1,0:T(8,128)}, f32[16,16,512]{2,1,0:T(8,128)}, f32[16,16,512]{2,1,0:T(8,128)}, f32[8,16,512]{2,1,0:T(8,128)}, f32[8,16,512]{2,...) custom-call(f32[4]{0:T(128)} %rigidity.1, ...), custom_call_target="tpu_custom_call" | custom-call | tf_op jit(solution)/shard_map/pallas_call | solution.py:123
  4.4 2.4 %collective-permute-start = (f32[12,16,512]{2,1,0:T(8,128)}, f32[12,16,512]{2,1,0:T(8,128)S(1)}, u32[]{:S(2)}, u32[]{:S(2)}) collective-permute-start(f32[12,16,512]{2,1,0:T(8,128)} %get-tuple-element.21), channel_id=1, source_target_pairs={{0,8},{8,16},{16,24},{1,9},{9,17},{17,25},{2,10},{10,18},{18,26},{... | collective-permute-start | bytes 1179656 | tf_op jit(solution)/shard_map/ppermute | solution.py:359
  6.8 1.3 %collective-permute-start.1 = (f32[12,16,512]{2,1,0:T(8,128)}, f32[12,16,512]{2,1,0:T(8,128)S(1)}, u32[]{:S(2)}, u32[]{:S(2)}) collective-permute-start(f32[12,16,512]{2,1,0:T(8,128)} %get-tuple-element.22), channel_id=1, source_target_pairs={{8,0},{16,8},{24,16},{9,1},{17,9},{25,17},{10,2},{18,10},{26,18},{... | collective-permute-start | bytes 1179656 | tf_op jit(solution)/shard_map/ppermute | solution.py:358
  8.1 4.2 %collective-permute-start.2 = (f32[8,16,512]{2,1,0:T(8,128)}, f32[8,16,512]{2,1,0:T(8,128)S(1)}, u32[]{:S(2)}, u32[]{:S(2)}) collective-permute-start(f32[8,16,512]{2,1,0:T(8,128)} %get-tuple-element.23.own_high), channel_id=1, source_target_pairs={{0,1},{1,2},{2,3},{3,4},{4,5},{5,6},{6,7},{8,9},{9,10},{10,11},{11... | collective-permute-start | bytes 786440 | tf_op jit(solution)/shard_map/ppermute | solution.py:359
  12.4 1.3 %collective-permute-start.3 = (f32[8,16,512]{2,1,0:T(8,128)}, f32[8,16,512]{2,1,0:T(8,128)S(1)}, u32[]{:S(2)}, u32[]{:S(2)}) collective-permute-start(f32[8,16,512]{2,1,0:T(8,128)} %get-tuple-element.24.own_low), channel_id=1, source_target_pairs={{1,0},{2,1},{3,2},{4,3},{5,4},{6,5},{7,6},{9,8},{10,9},{11,10},{12... | collective-permute-start | bytes 786440 | tf_op jit(solution)/shard_map/ppermute | solution.py:358
  13.7 4.6 %collective-permute-start.6 = (f32[4,16,512]{2,1,0:T(8,128)}, f32[4,16,512]{2,1,0:T(8,128)S(1)}, u32[]{:S(2)}, u32[]{:S(2)}) collective-permute-start(f32[4,16,512]{2,1,0:T(8,128)} %get-tuple-element.31), channel_id=1, source_target_pairs={{0,1},{1,2},{2,3},{3,4},{4,5},{5,6},{6,7},{8,9},{9,10},{10,11},{11... | collective-permute-start | bytes 393224 | tf_op jit(solution)/shard_map/ppermute | solution.py:359
  18.2 0.0 collective-permute-done.x_low
  18.2 0.0 copy-start
  18.2 1.3 %collective-permute-start.7 = (f32[4,16,512]{2,1,0:T(8,128)}, f32[4,16,512]{2,1,0:T(8,128)S(1)}, u32[]{:S(2)}, u32[]{:S(2)}) collective-permute-start(f32[4,16,512]{2,1,0:T(8,128)} %get-tuple-element.32), channel_id=1, source_target_pairs={{1,0},{2,1},{3,2},{4,3},{5,4},{6,5},{7,6},{9,8},{10,9},{11,10},{12... | collective-permute-start | bytes 393224 | tf_op jit(solution)/shard_map/ppermute | solution.py:358
  19.5 0.0 collective-permute-done.1.x_high
  19.6 0.0 copy-done
  19.6 0.0 copy-start.1
  19.6 0.7 %copy-done.1 = f32[12,16,512]{2,1,0:T(8,128)} copy-done((f32[12,16,512]{2,1,0:T(8,128)}, f32[12,16,512]{2,1,0:T(8,128)S(1)}, u32[]{:S(2)}) %copy-start.1) | copy-done | bytes 393240
  20.3 1.7 %shard_map.96 = (f32[24,512]{1,0:T(8,128)}, f32[24,512]{1,0:T(8,128)}) custom-call(f32[12,16,512]{2,1,0:T(8,128)} %copy-done, f32[12,16,512]{2,1,0:T(8,128)} %copy-done.1), custom_call_target="tpu_custom_call" | custom-call | tf_op jit(solution)/shard_map/pallas_call | solution.py:147
  22.0 5.0 %collective-permute-start.4 = (f32[24,512]{1,0:T(8,128)}, f32[24,512]{1,0:T(8,128)S(1)}, u32[]{:S(2)}, u32[]{:S(2)}) collective-permute-start(f32[24,512]{1,0:T(8,128)} %get-tuple-element.25), channel_id=1, source_target_pairs={{0,1},{1,2},{2,3},{3,4},{4,5},{5,6},{6,7},{8,9},{9,10},{10,11},{11... | collective-permute-start | bytes 147464 | tf_op jit(solution)/shard_map/ppermute | solution.py:359
  27.0 0.0 collective-permute-done.2.y_low
  27.0 0.0 copy-start.2
  27.0 1.3 %collective-permute-start.5 = (f32[24,512]{1,0:T(8,128)}, f32[24,512]{1,0:T(8,128)S(1)}, u32[]{:S(2)}, u32[]{:S(2)}) collective-permute-start(f32[24,512]{1,0:T(8,128)} %get-tuple-element.26), channel_id=1, source_target_pairs={{1,0},{2,1},{3,2},{4,3},{5,4},{6,5},{7,6},{9,8},{10,9},{11,10},{12... | collective-permute-start | bytes 147464 | tf_op jit(solution)/shard_map/ppermute | solution.py:358
  28.3 0.0 collective-permute-done.3.y_high
  28.3 2.2 %collective-permute-done.4.c_low = f32[24,512]{1,0:T(8,128)S(1)} collective-permute-done((f32[24,512]{1,0:T(8,128)}, f32[24,512]{1,0:T(8,128)S(1)}, u32[]{:S(2)}, u32[]{:S(2)}) %collective-permute-start.4) | collective-permute-done | bytes 49184 | tf_op jit(solution)/shard_map/ppermute | solution.py:359
  30.5 3.6 %collective-permute-done.5.c_high = f32[24,512]{1,0:T(8,128)S(1)} collective-permute-done((f32[24,512]{1,0:T(8,128)}, f32[24,512]{1,0:T(8,128)S(1)}, u32[]{:S(2)}, u32[]{:S(2)}) %collective-permute-start.5) | collective-permute-done | bytes 49184 | tf_op jit(solution)/shard_map/ppermute | solution.py:358
  34.1 0.6 copy-done.7
  34.7 8.4 %shard_map.97 = (f32[3,16,16,512]{3,2,1,0:T(8,128)}, f32[6,16,512]{2,1,0:T(8,128)}, f32[6,16,512]{2,1,0:T(8,128)}, f32[32,128]{1,0:T(8,128)}) custom-call(f32[3,16,16,512]{3,2,1,0:T(8,128)} %motion.5, f32[16,16,512]{2,1,0:T(8,128)} %get-tuple-element.20.half, f32[12,16,512]{2,1,0:T(8,128)} %copy-done, f32[12,16,512]{2,1,0:T(8,128)} %copy-done.1, ...), custom_call_target="tpu_custom_call" | custom-call | tf_op jit(solution)/shard_map/pallas_call | solution.py:369
  43.1 8.8 %all-to-all-start = ((f32[32,1,128]{2,1,0:T(1,128)}), f32[32,1,128]{2,1,0:T(1,128)S(1)}, u32[]{:S(2)}, u32[]{:S(2)}) async-start(f32[32,1,128]{2,1,0:T(1,128)} %bitcast.5), calls=%async_computation | async-start | bytes 32768 | tf_op jit(solution)/shard_map/all_to_all | solution.py:374
  51.9 0.0 collective-permute-done.6.late_low
  51.9 0.0 collective-permute-done.7.late_high
  51.9 0.6 copy-done.4
  52.5 0.7 copy-done.5
  53.2 2.3 %shard_map.98 = (f32[2,16,512]{2,1,0:T(8,128)}, f32[2,16,512]{2,1,0:T(8,128)}, f32[8,512]{1,0:T(8,128)}) custom-call(f32[12,16,512]{2,1,0:T(8,128)} %copy-done, f32[12,16,512]{2,1,0:T(8,128)} %copy-done.1, f32[8,16,512]{2,1,0:T(8,128)} %copy-done.2, f32[8,16,512]{2,1,0:T(8,128)} %copy-done.3, f32[4,16,512]{2,1,0:T(8,128)} %copy-done.4, ...), custom_call_target="tpu_custom_call" | custom-call | tf_op jit(solution)/shard_map/pallas_call | solution.py:375
  55.5 3.5 %all-to-all-done = f32[32,1,128]{2,1,0:T(1,128)S(1)} async-done(((f32[32,1,128]{2,1,0:T(1,128)}), f32[32,1,128]{2,1,0:T(1,128)S(1)}, u32[]{:S(2)}, u32[]{:S(2)}) %all-to-all-start) | async-done | bytes 16416 | tf_op jit(solution)/shard_map/all_to_all | solution.py:374
  59.0 0.6 copy-done.8
  59.6 7.8 %shard_map.99 = (f32[3,16,16,512]{3,2,1,0:T(8,128)}, f32[16,16,512]{2,1,0:T(8,128)}) custom-call(f32[32,128]{1,0:T(8,128)} %bitcast.4, f32[3,16,16,512]{3,2,1,0:T(8,128)} %motion.5, f32[3,16,16,512]{3,2,1,0:T(8,128)} %get-tuple-element.28.q, f32[16,16,512]{2,1,0:T(8,128)} %get-tuple-element.29.kappa, f32[16,16,512]{2,1,0:T(8,128)} %get-tuple-element.30.links, ...), custom_call_target="tpu_custom_call" | custom-call | tf_op jit(solution)/shard_map/pallas_call | solution.py:378
  (9 shorter events, 0.0 us)
Async XLA Ops:
  4.4 13.8 %collective-permute-start = (f32[12,16,512]{2,1,0:T(8,128)}, f32[12,16,512]{2,1,0:T(8,128)S(1)}, u32[]{:S(2)}, u32[]{:S(2)}) collective-permute-start(f32[12,16,512]{2,1,0:T(8,128)} %get-tuple-element.21), channel_id=1, source_target_pairs={{0,8},{8,16},{16,24},{1,9},{9,17},{17,25},{2,10},{10,18},{18,26},{... | collective-permute-start | bytes 1179656 | tf_op jit(solution)/shard_map/ppermute | solution.py:359
  6.8 12.7 %collective-permute-start.1 = (f32[12,16,512]{2,1,0:T(8,128)}, f32[12,16,512]{2,1,0:T(8,128)S(1)}, u32[]{:S(2)}, u32[]{:S(2)}) collective-permute-start(f32[12,16,512]{2,1,0:T(8,128)} %get-tuple-element.22), channel_id=1, source_target_pairs={{8,0},{16,8},{24,16},{9,1},{17,9},{25,17},{10,2},{18,10},{26,18},{... | collective-permute-start | bytes 1179656 | tf_op jit(solution)/shard_map/ppermute | solution.py:358
  8.1 18.8 %collective-permute-start.2 = (f32[8,16,512]{2,1,0:T(8,128)}, f32[8,16,512]{2,1,0:T(8,128)S(1)}, u32[]{:S(2)}, u32[]{:S(2)}) collective-permute-start(f32[8,16,512]{2,1,0:T(8,128)} %get-tuple-element.23.own_high), channel_id=1, source_target_pairs={{0,1},{1,2},{2,3},{3,4},{4,5},{5,6},{6,7},{8,9},{9,10},{10,11},{11... | collective-permute-start | bytes 786440 | tf_op jit(solution)/shard_map/ppermute | solution.py:359
  12.4 15.9 %collective-permute-start.3 = (f32[8,16,512]{2,1,0:T(8,128)}, f32[8,16,512]{2,1,0:T(8,128)S(1)}, u32[]{:S(2)}, u32[]{:S(2)}) collective-permute-start(f32[8,16,512]{2,1,0:T(8,128)} %get-tuple-element.24.own_low), channel_id=1, source_target_pairs={{1,0},{2,1},{3,2},{4,3},{5,4},{6,5},{7,6},{9,8},{10,9},{11,10},{12... | collective-permute-start | bytes 786440 | tf_op jit(solution)/shard_map/ppermute | solution.py:358
  13.7 38.2 %collective-permute-start.6 = (f32[4,16,512]{2,1,0:T(8,128)}, f32[4,16,512]{2,1,0:T(8,128)S(1)}, u32[]{:S(2)}, u32[]{:S(2)}) collective-permute-start(f32[4,16,512]{2,1,0:T(8,128)} %get-tuple-element.31), channel_id=1, source_target_pairs={{0,1},{1,2},{2,3},{3,4},{4,5},{5,6},{6,7},{8,9},{9,10},{10,11},{11... | collective-permute-start | bytes 393224 | tf_op jit(solution)/shard_map/ppermute | solution.py:359
  18.2 1.3 %copy-start = (f32[12,16,512]{2,1,0:T(8,128)}, f32[12,16,512]{2,1,0:T(8,128)S(1)}, u32[]{:S(2)}) copy-start(f32[12,16,512]{2,1,0:T(8,128)S(1)} %collective-permute-done.x_low) | copy-start | bytes 1179652
  18.2 33.7 %collective-permute-start.7 = (f32[4,16,512]{2,1,0:T(8,128)}, f32[4,16,512]{2,1,0:T(8,128)S(1)}, u32[]{:S(2)}, u32[]{:S(2)}) collective-permute-start(f32[4,16,512]{2,1,0:T(8,128)} %get-tuple-element.32), channel_id=1, source_target_pairs={{1,0},{2,1},{3,2},{4,3},{5,4},{6,5},{7,6},{9,8},{10,9},{11,10},{12... | collective-permute-start | bytes 393224 | tf_op jit(solution)/shard_map/ppermute | solution.py:358
  19.6 0.8 %copy-start.1 = (f32[12,16,512]{2,1,0:T(8,128)}, f32[12,16,512]{2,1,0:T(8,128)S(1)}, u32[]{:S(2)}) copy-start(f32[12,16,512]{2,1,0:T(8,128)S(1)} %collective-permute-done.1.x_high) | copy-start | bytes 1179652
  22.0 8.5 %collective-permute-start.4 = (f32[24,512]{1,0:T(8,128)}, f32[24,512]{1,0:T(8,128)S(1)}, u32[]{:S(2)}, u32[]{:S(2)}) collective-permute-start(f32[24,512]{1,0:T(8,128)} %get-tuple-element.25), channel_id=1, source_target_pairs={{0,1},{1,2},{2,3},{3,4},{4,5},{5,6},{6,7},{8,9},{9,10},{10,11},{11... | collective-permute-start | bytes 147464 | tf_op jit(solution)/shard_map/ppermute | solution.py:359
  27.0 7.1 %copy-start.2 = (f32[8,16,512]{2,1,0:T(8,128)}, f32[8,16,512]{2,1,0:T(8,128)S(1)}, u32[]{:S(2)}) copy-start(f32[8,16,512]{2,1,0:T(8,128)S(1)} %collective-permute-done.2.y_low) | copy-start | bytes 786436
  27.0 7.1 %collective-permute-start.5 = (f32[24,512]{1,0:T(8,128)}, f32[24,512]{1,0:T(8,128)S(1)}, u32[]{:S(2)}, u32[]{:S(2)}) collective-permute-start(f32[24,512]{1,0:T(8,128)} %get-tuple-element.26), channel_id=1, source_target_pairs={{1,0},{2,1},{3,2},{4,3},{5,4},{6,5},{7,6},{9,8},{10,9},{11,10},{12... | collective-permute-start | bytes 147464 | tf_op jit(solution)/shard_map/ppermute | solution.py:358
  28.3 5.8 %copy-start.3 = (f32[8,16,512]{2,1,0:T(8,128)}, f32[8,16,512]{2,1,0:T(8,128)S(1)}, u32[]{:S(2)}) copy-start(f32[8,16,512]{2,1,0:T(8,128)S(1)} %collective-permute-done.3.y_high) | copy-start | bytes 786436
  30.5 3.6 %copy-start.6 = (f32[24,512]{1,0:T(8,128)}, f32[24,512]{1,0:T(8,128)S(1)}, u32[]{:S(2)}) copy-start(f32[24,512]{1,0:T(8,128)S(1)} %collective-permute-done.4.c_low) | copy-start | bytes 147460
  34.1 0.6 copy-start.7
  43.1 15.8 %all-to-all-start = ((f32[32,1,128]{2,1,0:T(1,128)}), f32[32,1,128]{2,1,0:T(1,128)S(1)}, u32[]{:S(2)}, u32[]{:S(2)}) async-start(f32[32,1,128]{2,1,0:T(1,128)} %bitcast.5), calls=%async_computation | async-start | bytes 32768 | tf_op jit(solution)/shard_map/all_to_all | solution.py:374
  51.9 0.6 copy-start.4
  52.5 0.7 copy-start.5
  59.0 0.6 copy-start.8
